TPU v7x, 1024 devices: a whole 4x4x32 slice. The times are simulated.
1024 devices in a mesh: sec: 2 (over core), tile: 512 (over x, z, y).
Axes of the slice: x: 4, y: 4, z: 32, core: 2. Of those that a mesh axis runs over, the one named last changes fastest.
Arguments:
- object_field: bfloat16 [2, 2, 131072, 512], P(None, 'sec', 'tile'), may hold values from -1 to 1
- probe: bfloat16 [2, 256, 256], replicated, may hold values from -6 to 6
- phases: float32 [256], replicated, may hold values from -3.140625 to 3.140625
- intensities: bfloat16 [1024, 256, 256], P('tile'), may hold values from 0.099609375 to 2
- pos_row: int32 [1024], P('tile'), may hold values from 0 to 255
- pos_col: int32 [1024], P('tile'), may hold values from 0 to 256
- counts: int32 [512], P('tile'), may hold values from 1 to 2, as said below
Outputs:
- object_gradient: float32 [2, 2, 131072, 512], P(None, 'sec', 'tile')
Inputs may be any that keep to these rules, and one draw needn't show every extreme that they name: `counts`: every strip has at least one live position, and some strip has exactly 2 in every draw.
All inputs are finite; a program needn't handle non-finite values.
Results may differ from a plain program's by a relative error of at most 0.025.
Values may be sent and summed in bfloat16 or wider, within the bound.
A program may use at most 64 MiB of HBM per device.

v0:
```python
import math

import jax
import jax.numpy as jnp
from jax import lax
from jax.sharding import PartitionSpec as P


def shifted(value, axis, steps):
    count = lax.axis_size(axis)
    first, last = (max(0, -steps), min(count, count - steps))
    return lax.ppermute(value, axis, [(source, source + steps) for source in range(first, last)])


def build_tables(phases, wave_side):
    frequency = jnp.arange(wave_side, dtype=jnp.int32)
    product = frequency[:, None] * frequency[None, :] % wave_side
    angles = product.astype(jnp.float32) * (2.0 * math.pi / wave_side)
    cosine = jnp.cos(angles)
    sine_table = jnp.sin(angles)
    turned = phases[:, None] + angles
    turned_re = jnp.cos(turned)
    turned_im = jnp.sin(turned)
    highest = lax.Precision.HIGHEST
    kernel_re = (
        jnp.dot(turned_re.T, cosine, precision=highest, preferred_element_type=jnp.float32)
        + jnp.dot(turned_im.T, sine_table, precision=highest, preferred_element_type=jnp.float32)
    ) / wave_side
    kernel_im = (
        jnp.dot(turned_im.T, cosine, precision=highest, preferred_element_type=jnp.float32)
        - jnp.dot(turned_re.T, sine_table, precision=highest, preferred_element_type=jnp.float32)
    ) / wave_side
    norm_scale = 1.0 / math.sqrt(wave_side)
    far_re = cosine * norm_scale
    far_im = -sine_table * norm_scale
    return (
        kernel_re.astype(jnp.bfloat16),
        kernel_im.astype(jnp.bfloat16),
        far_re.astype(jnp.bfloat16),
        far_im.astype(jnp.bfloat16),
    )


def left_product(matrix, field):
    return jnp.einsum("mj,bjn->bmn", matrix, field, preferred_element_type=jnp.float32)


def right_product(field, matrix):
    return jnp.einsum("bmj,nj->bmn", field, matrix, preferred_element_type=jnp.float32)


def propagate(matrix_re, matrix_im, field_re, field_im):
    inner_re = (left_product(matrix_re, field_re) - left_product(matrix_im, field_im)).astype(
        jnp.bfloat16
    )
    inner_im = (left_product(matrix_re, field_im) + left_product(matrix_im, field_re)).astype(
        jnp.bfloat16
    )
    outer_re = (right_product(inner_re, matrix_re) - right_product(inner_im, matrix_im)).astype(
        jnp.bfloat16
    )
    outer_im = (right_product(inner_re, matrix_im) + right_product(inner_im, matrix_re)).astype(
        jnp.bfloat16
    )
    return (outer_re, outer_im)


def transmit(trans_re, trans_im, wave_re, wave_im):
    t_re = trans_re.astype(jnp.float32)
    t_im = trans_im.astype(jnp.float32)
    w_re = wave_re.astype(jnp.float32)
    w_im = wave_im.astype(jnp.float32)
    return (
        (t_re * w_re - t_im * w_im).astype(jnp.bfloat16),
        (t_re * w_im + t_im * w_re).astype(jnp.bfloat16),
    )


def conj_times(first_re, first_im, second_re, second_im):
    a_re = first_re.astype(jnp.float32)
    a_im = first_im.astype(jnp.float32)
    b_re = second_re.astype(jnp.float32)
    b_im = second_im.astype(jnp.float32)
    return (a_re * b_re + a_im * b_im, a_re * b_im - a_im * b_re)


def on_device(object_field, probe, phases, intensities, pos_row, pos_col, counts):
    slot_count = pos_row.shape[0]
    layer_count = object_field.shape[1]
    strip_rows = object_field.shape[2]
    wave_side = probe.shape[1]
    section = lax.axis_index("sec")
    sections = lax.axis_size("sec")
    first_section = section == 0
    last_section = section == sections - 1
    next_strip = shifted(object_field, "tile", -1)
    extended = jnp.concatenate([object_field, next_strip], axis=2)
    kernel_re, kernel_im, far_re, far_im = build_tables(phases, wave_side)
    live_slots = counts[0]
    anchor = jnp.zeros((), jnp.int32)
    forward_mats = []
    layer_index = 0
    forward_mats.append(
        (jnp.where(last_section, far_re, kernel_re), jnp.where(last_section, far_im, kernel_im))
    )
    adjoint_mats = [(matrix_pair[0].T, -matrix_pair[1].T) for matrix_pair in forward_mats]
    per_step = 1
    groups = slot_count // per_step

    def windows_of(group_index):
        top_rows = lax.dynamic_slice_in_dim(pos_row, group_index * per_step, per_step)
        left_cols = lax.dynamic_slice_in_dim(pos_col, group_index * per_step, per_step)

        def cut_window(top_row, left_col):
            return lax.dynamic_slice(
                extended,
                (anchor, anchor, top_row, left_col),
                (2, layer_count, wave_side, wave_side),
            )

        return (jax.vmap(cut_window)(top_rows, left_cols), top_rows, left_cols)

    def forward(group_index, wave_re, wave_im, stored):
        windows, top_rows, left_cols = windows_of(group_index)
        entries = [jnp.stack([wave_re, wave_im], axis=1)]
        mixed_re, mixed_im = transmit(windows[:, 0, 0], windows[:, 1, 0], wave_re, wave_im)
        wave_re, wave_im = propagate(forward_mats[0][0], forward_mats[0][1], mixed_re, mixed_im)
        stored = lax.dynamic_update_slice_in_dim(
            stored, jnp.stack(entries, axis=1)[None], group_index, 0
        )
        return (stored, jnp.stack([wave_re, wave_im], axis=1))

    def backward(group_index, back_re, back_im, stored, gradient):
        windows, top_rows, left_cols = windows_of(group_index)
        entries = lax.dynamic_index_in_dim(stored, group_index, 0, keepdims=False)
        patch_re = [None] * layer_count
        patch_im = [None] * layer_count
        for layer_index in reversed(range(layer_count)):
            matrix_re, matrix_im = adjoint_mats[layer_index]
            spread_re, spread_im = propagate(matrix_re, matrix_im, back_re, back_im)
            patch_re[layer_index], patch_im[layer_index] = conj_times(
                entries[:, layer_index, 0], entries[:, layer_index, 1], spread_re, spread_im
            )
            next_re, next_im = conj_times(
                windows[:, 0, layer_index], windows[:, 1, layer_index], spread_re, spread_im
            )
            back_re = next_re.astype(jnp.bfloat16)
            back_im = next_im.astype(jnp.bfloat16)
        patches = jnp.stack([jnp.stack(patch_re, axis=1), jnp.stack(patch_im, axis=1)], axis=1)
        corner = (anchor, anchor, top_rows[0], left_cols[0])
        current = lax.dynamic_slice(gradient, corner, (2, layer_count, wave_side, wave_side))
        gradient = lax.dynamic_update_slice(gradient, current + patches[0], corner)
        return (gradient, jnp.stack([back_re, back_im], axis=1))

    probe_wave = probe[None]

    def advance(step_index, carried, send_down, send_up):
        stored, gradient, from_above, from_below = carried
        front_group = step_index - section
        rear_group = step_index - 2 * (sections - 1) + section
        front_ok = (front_group >= 0) & (front_group < groups)
        rear_ok = (rear_group >= 0) & (rear_group < groups)
        front_at = jnp.clip(front_group, 0, groups - 1)
        rear_at = jnp.clip(rear_group, 0, groups - 1)
        start_wave = jnp.where(first_section, probe_wave, from_above)
        stored, leaving = lax.cond(
            front_ok,
            lambda saved_in: forward(front_at, start_wave[:, 0], start_wave[:, 1], saved_in),
            lambda saved_in: (saved_in, jnp.zeros_like(start_wave)),
            stored,
        )
        measured = lax.dynamic_slice_in_dim(intensities, front_at * per_step, per_step, 0).astype(
            jnp.float32
        )
        slot_ids = front_at * per_step + jnp.arange(per_step, dtype=jnp.int32)
        weights = (slot_ids < live_slots).astype(jnp.float32)
        leave_re = leaving[:, 0].astype(jnp.float32)
        leave_im = leaving[:, 1].astype(jnp.float32)
        factor = (
            2.0 * (leave_re * leave_re + leave_im * leave_im - measured) * weights[:, None, None]
        )
        residual = jnp.stack([factor * leave_re, factor * leave_im], axis=1).astype(jnp.bfloat16)
        arriving = jnp.where(last_section, residual, from_below)
        gradient, returning = lax.cond(
            rear_ok,
            lambda grad_in: backward(rear_at, arriving[:, 0], arriving[:, 1], stored, grad_in),
            lambda grad_in: (grad_in, jnp.zeros_like(arriving)),
            gradient,
        )
        if send_down:
            from_above = shifted(leaving, "sec", 1)
        if send_up:
            from_below = shifted(returning, "sec", -1)
        return (stored, gradient, from_above, from_below)

    carried = (
        jnp.zeros((groups, per_step, layer_count, 2, wave_side, wave_side), jnp.bfloat16),
        jnp.zeros((2, layer_count, 2 * strip_rows, object_field.shape[3]), jnp.float32),
        jnp.zeros((per_step, 2, wave_side, wave_side), jnp.bfloat16),
        jnp.zeros((per_step, 2, wave_side, wave_side), jnp.bfloat16),
    )
    carried = advance(0, carried, True, False)
    carried = lax.fori_loop(
        1,
        groups + 1,
        lambda step_index, inner_state: advance(step_index, inner_state, True, True),
        carried,
    )
    carried = advance(groups + 1, carried, False, False)
    gradient = carried[1]
    arrived = shifted(gradient[:, :, strip_rows:].astype(jnp.bfloat16), "tile", 1).astype(
        jnp.float32
    )
    return gradient[:, :, :strip_rows] + arrived


def solution(mesh):
    placed = (
        P(None, "sec", "tile", None),
        P(),
        P(),
        P("tile", None, None),
        P("tile"),
        P("tile"),
        P("tile"),
    )
    return jax.shard_map(
        on_device,
        mesh=mesh,
        in_specs=placed,
        out_specs=P(None, "sec", "tile", None),
        check_vma=False,
    )
```

profile of v0, /device:TPU:6, one launch (start us, length us, event | category | flops | bytes accessed | tf_op | source)
XLA Modules:
  0.0 158.6 jit_solution(12648129650058422800)
XLA Ops:
  0.0 21.5 %collective-permute-start.2 = (bf16[2,1,256,512]{3,2,0,1:T(8,128)(2,1)}, bf16[2,1,256,512]{3,2,0,1:T(8,128)(2,1)S(1)}, u32[]{:S(2)}, u32[]{:S(2)}) collective-permute-start(bf16[2,1,256,512]{3,2,0,1:T(8,128)(2,1)} %bitcast.458), channel_id=1, source_target_pairs={{1,0},{2,1},{3,2},{4,3},{5,4},{6,5},{7,6},{8,7},{9,8},{10,9},{11,1... | collective-permute-start | bytes 1572872 | tf_op jit(solution)/shard_map/ppermute | solution.py:12
  21.5 1.0 broadcast_multiply_fusion
  22.5 3.1 %fusion.114 = f32[256,256]{1,0:T(8,128)S(1)} fusion(f32[256]{0:T(256)} %param.23), kind=kOutput, calls=%fused_computation.239 | convolution fusion | flops 203227136 | bytes 263168 | tf_op jit(solution)/shard_map/dot_general | solution.py:26
  25.6 2.4 %fusion.115 = f32[256,256]{1,0:T(8,128)S(1)} fusion(f32[256]{0:T(256)S(1)} %copy-done.4), kind=kOutput, calls=%fused_computation.240 | convolution fusion | flops 203227136 | bytes 263168 | tf_op jit(solution)/shard_map/dot_general | solution.py:30
  28.0 2.4 %fusion.96 = bf16[256,256]{1,0:T(8,128)(2,1)S(1)} fusion(f32[256,256]{1,0:T(8,128)S(1)} %fusion.114, f32[256]{0:T(256)S(1)} %copy-done.4), kind=kOutput, calls=%fused_computation.202 | convolution fusion | flops 203423744 | bytes 394240 | tf_op jit(solution)/shard_map/dot_general | solution.py:27
  30.4 2.4 %broadcast_select_fusion.4 = (bf16[256,256]{1,0:T(8,128)(2,1)S(1)}, bf16[256,256]{1,0:T(8,128)(2,1)S(1)}) fusion(pred[]{:T(512)} %eq.9, f32[256,256]{1,0:T(8,128)S(1)} %fusion.115, f32[256]{0:T(256)S(1)} %copy-done.4), kind=kOutput, calls=%fused_computation.255 | convolution fusion | flops 204603392 | bytes 525313 | tf_op jit(solution)/shard_map/dot_general | solution.py:31
  32.8 1.0 multiply_convert_fusion
  34.7 0.3 copy.14
  35.1 0.7 bitcast_select_fusion.1
  35.8 1.0 copy.17
  37.1 13.2 %conditional.6 = (bf16[2,1,1,2,256,256]{5,4,3,2,1,0:T(8,128)(2,1)}, bf16[1,2,256,256]{3,2,1,0:T(8,128)(2,1)}) conditional(s32[]{:T(128)} %convert_element_type.747, () %tuple.99, (pred[]{:T(512)}, bf16[2,256,256]{2,1,0:T(8,128)(2,1)S(1)}, s32[]{:T(128)}, s32[2]{0:T(128)S(1)}, s32[2]{0:T(128)S(1)}, /*index=5*/bf16[2,1,512,512]{3,2,0,1:T(8,128)(2,1)S(1)}, ...), branch_computations={%region_0.1_spmd, %region_1.2_spmd} | conditional | flops 270139392 | bytes 8127133 | solution.py:166
  37.1 0.6 dynamic_slice.51
  39.7 0.6 dynamic_slice.52
  42.5 1.1 fusion.155
  43.9 1.1 fusion.156
  45.0 1.1 fusion.157
  46.8 1.1 fusion.33
  48.0 0.7 pad_maximum_fusion
  48.7 0.8 broadcast_in_dim.27
  49.5 0.7 bitcast_dynamic-update-slice_fusion
  50.3 1.3 collective-permute-start.3
  51.6 1.1 fusion.117
  52.8 0.7 select_n.199
  53.5 1.6 %conditional.7 = (f32[2,1,512,512]{3,2,0,1:T(8,128)}) conditional(s32[]{:T(128)} %convert_element_type.753, () %tuple.101, (s32[]{:T(128)}, bf16[2,1,1,2,256,256]{5,4,3,2,1,0:T(8,128)(2,1)}, pred[1,2,256,256]{3,2,1,0:T(8,128)(4,1)}, bf16[1,2,256,256]{3,2,1,0:T(8,128)(2,1)S(1)}, bf16[1,2,256,256]{3,2,1,0:T(8,128)(2,1)S(1)}, ...), branch_computations={%region_2.3_spmd, %region_3.4_spmd} | conditional | bytes 12189832 | solution.py:184
  53.5 1.6 %broadcast_in_dim.38 = f32[2,1,512,512]{3,2,0,1:T(8,128)} broadcast(f32[]{:T(128)} %constant.147.clone), dimensions={} | broadcast | bytes 2097156 | tf_op jit(solution)/shard_map/broadcast_in_dim | solution.py:198
  55.1 66.4 %while.39 = (s32[]{:T(128)}, bf16[2,1,1,2,256,256]{5,4,3,2,1,0:T(8,128)(2,1)}, f32[2,1,512,512]{3,2,0,1:T(8,128)}, bf16[1,2,256,256]{3,2,1,0:T(8,128)(2,1)S(1)},...) while((s32[]{:T(128)}, ...), condition=%wide.region_9.10_spmd, body=%wide.region_4.9_spmd.sunk | while | flops 541720576 | bytes 22152668 | solution.py:203
  55.1 8.0 %conditional.12 = (bf16[2,1,1,2,256,256]{5,4,3,2,1,0:T(8,128)(2,1)}, bf16[1,2,256,256]{3,2,1,0:T(8,128)(2,1)S(1)}) conditional(s32[]{:T(128)} %convert_element_type.968, bf16[2,1,1,2,256,256]{5,4,3,2,1,0:T(8,128)(2,1)} %get-tuple-element.1119, (pred[]{:T(512)}, bf16[1,2,256,256]{3,2,1,0:T(8,128)(2,1)S(1)}, bf16[1,2,256,256]{3,2,1,0:T(8,128)(2,1)S(1)}, ...), branch_computations={%region_5.5_spmd, %region_6.6_spmd} | conditional | flops 270008320 | bytes 7602842 | solution.py:166
  55.1 0.6 dynamic_slice.56
  57.8 0.6 dynamic_slice.57
  60.3 0.8 bitcast_dynamic-update-slice_fusion.1
  61.4 0.2 fusion.48
  61.9 0.2 fusion.49
  62.4 0.2 fusion.47
  63.8 1.0 fusion.254
  64.8 0.7 conditional.13
  64.8 0.7 broadcast.84
  65.6 1.3 collective-permute-start.1
  66.8 19.1 %collective-permute-start = (bf16[1,2,256,256]{3,2,1,0:T(8,128)(2,1)S(1)}, bf16[1,2,256,256]{3,2,1,0:T(8,128)(2,1)S(1)}, u32[]{:S(2)}, u32[]{:S(2)}) collective-permute-start(bf16[1,2,256,256]{3,2,1,0:T(8,128)(2,1)S(1)} %get-tuple-element.1077), channel_id=1, source_target_pairs={{0,512},{1,513},{2,514},{3,515},{4,516},{5,517},{6,518},{7,519},{8... | collective-permute-start | bytes 786440 | tf_op jit(solution)/shard_map/while/body/eval_jaxpr/ppermute | solution.py:12
  86.0 1.1 collective-permute-done
  87.8 1.0 fusion.254
  88.8 19.7 %conditional.13 = (f32[2,1,512,512]{3,2,0,1:T(8,128)}, bf16[1,2,256,256]{3,2,1,0:T(8,128)(2,1)}) conditional(s32[]{:T(128)} %convert_element_type.969, f32[2,1,512,512]{3,2,0,1:T(8,128)} %get-tuple-element.1120, (s32[]{:T(128)}, s32[2]{0:T(128)S(1)}, s32[2]{0:T(128)S(1)}, f32[2,1,512,512]{3,2,0,1:T(8,128)}, ...), branch_computations={%region_7.7_spmd, %region_8.8_spmd} | conditional | flops 270794752 | bytes 11272417 | solution.py:184
  90.3 0.6 dynamic_slice.58
  92.6 0.6 dynamic_slice.59
  95.3 1.0 dynamic-slice_bitcast_fusion.5
  96.2 0.3 fusion.72
  96.6 0.7 pad_maximum_fusion.2
  100.7 1.4 fusion.62
  102.1 6.5 %dynamic_update_slice.15 = f32[2,1,512,512]{3,2,0,1:T(8,128)} dynamic-update-slice(f32[2,1,512,512]{3,2,0,1:T(8,128)} %get-tuple-element.726, f32[2,1,256,256]{3,2,0,1:T(8,128)S(1)} %fusion.62, s32[]{:T(128)} %constant.162.clone, s32[]{:T(128)} %constant.162.clone, s32[]{:T(128)S(6)} %select_n.165, s32[]{:T(128)S(6)} %select_n.166) | dynamic-update-slice | bytes 1048580 | tf_op jit(solution)/shard_map/while/body/eval_jaxpr/cond/branch_1_fun/dynamic_update_slice | solution.py:152
  108.6 1.3 collective-permute-start.1
  109.9 10.5 %collective-permute-start = (bf16[1,2,256,256]{3,2,1,0:T(8,128)(2,1)S(1)}, bf16[1,2,256,256]{3,2,1,0:T(8,128)(2,1)S(1)}, u32[]{:S(2)}, u32[]{:S(2)}) collective-permute-start(bf16[1,2,256,256]{3,2,1,0:T(8,128)(2,1)S(1)} %get-tuple-element.1077), channel_id=1, source_target_pairs={{0,512},{1,513},{2,514},{3,515},{4,516},{5,517},{6,518},{7,519},{8... | collective-permute-start | bytes 786440 | tf_op jit(solution)/shard_map/while/body/eval_jaxpr/ppermute | solution.py:12
  120.4 1.1 collective-permute-done
  121.5 1.0 fusion.116
  122.6 17.1 %conditional.9 = (f32[2,1,512,512]{3,2,0,1:T(8,128)}) conditional(s32[]{:T(128)} %convert_element_type.746, f32[2,1,512,512]{3,2,0,1:T(8,128)} %get-tuple-element.790, (s32[]{:T(128)}, s32[2]{0:T(128)S(1)}, s32[2]{0:T(128)S(1)}, f32[2,1,512,512]{3,2,0,1:T(8,128)}, bf16[2,1,1,2,256,256]{5,4,3,2,1,0:T(8,128)(2,1)}, ...), branch_computations={%region_12.13_spmd, %region_13.14_spmd} | conditional | flops 270008320 | bytes 9830540 | solution.py:184
  122.6 1.0 select_n.179
  125.2 1.0 dynamic-slice_bitcast_fusion.1
  126.2 0.3 fusion.24
  126.5 0.7 dynamic_slice.65
  129.0 0.7 dynamic_slice.66
  131.6 1.4 fusion.22
  133.0 6.7 %dynamic_update_slice.17 = f32[2,1,512,512]{3,2,0,1:T(8,128)} dynamic-update-slice(f32[2,1,512,512]{3,2,0,1:T(8,128)} %get-tuple-element.770, f32[2,1,256,256]{3,2,0,1:T(8,128)S(1)} %fusion.22, s32[]{:T(128)} %constant.181.clone, s32[]{:T(128)} %constant.181.clone, s32[]{:T(128)S(6)} %select_n.177, s32[]{:T(128)S(6)} %select_n.178) | dynamic-update-slice | bytes 1048580 | tf_op jit(solution)/shard_map/cond/branch_1_fun/dynamic_update_slice | solution.py:152
  139.7 1.3 slice.376
  141.0 1.9 %collective-permute-start.4 = (bf16[2,1,256,512]{3,2,1,0:T(8,128)(2,1)S(1)}, bf16[2,1,256,512]{3,2,1,0:T(8,128)(2,1)S(1)}, u32[]{:S(2)}, u32[]{:S(2)}) collective-permute-start(bf16[2,1,256,512]{3,2,1,0:T(8,128)(2,1)S(1)} %slice.376), channel_id=1, source_target_pairs={{0,1},{1,2},{2,3},{3,4},{4,5},{5,6},{6,7},{7,8},{8,9},{9,10},{10,1... | collective-permute-start | bytes 1572872 | tf_op jit(solution)/shard_map/ppermute | solution.py:12
  142.9 13.4 %collective-permute-done.4 = bf16[2,1,256,512]{3,2,1,0:T(8,128)(2,1)S(1)} collective-permute-done((bf16[2,1,256,512]{3,2,1,0:T(8,128)(2,1)S(1)}, bf16[2,1,256,512]{3,2,1,0:T(8,128)(2,1)S(1)}, u32[]{:S(2)}, u32[]{:S(2)}) %collective-permute-start.4) | collective-permute-done | bytes 524320 | tf_op jit(solution)/shard_map/ppermute | solution.py:12
  156.3 2.4 %slice_add_fusion = f32[2,1,256,512]{3,2,1,0:T(8,128)} fusion(f32[2,1,512,512]{3,2,1,0:T(8,128)} %bitcast.174, bf16[2,1,256,512]{3,2,1,0:T(8,128)(2,1)S(1)} %collective-permute-done.4), kind=kLoop, calls=%fused_computation.205 | loop fusion | flops 524288 | bytes 2621440 | tf_op jit(solution)/shard_map/add | solution.py:214
  (64 shorter events, 6.7 us)
Async XLA Ops:
  0.0 25.6 %copy-start.4 = (f32[256]{0:T(256)S(1)}, f32[256]{0:T(256)}, u32[]{:S(2)}) copy-start(f32[256]{0:T(256)} %param.23) | copy-start | bytes 3076
  0.0 37.0 %collective-permute-start.2 = (bf16[2,1,256,512]{3,2,0,1:T(8,128)(2,1)}, bf16[2,1,256,512]{3,2,0,1:T(8,128)(2,1)S(1)}, u32[]{:S(2)}, u32[]{:S(2)}) collective-permute-start(bf16[2,1,256,512]{3,2,0,1:T(8,128)(2,1)} %bitcast.458), channel_id=1, source_target_pairs={{1,0},{2,1},{3,2},{4,3},{5,4},{6,5},{7,6},{8,7},{9,8},{10,9},{11,1... | collective-permute-start | bytes 1572872 | tf_op jit(solution)/shard_map/ppermute | solution.py:12
  32.8 4.2 %copy-start.3 = (bf16[2,1,256,512]{3,2,1,0:T(8,128)(2,1)S(1)}, bf16[2,1,256,512]{3,2,1,0:T(8,128)(2,1)}, u32[]{:S(2)}) copy-start(bf16[2,1,256,512]{3,2,1,0:T(8,128)(2,1)} %param.21) | copy-start | bytes 1572868
  34.7 2.4 %copy-start = (bf16[2,256,256]{2,1,0:T(8,128)(2,1)S(1)}, bf16[2,256,256]{2,1,0:T(8,128)(2,1)}, u32[]{:S(2)}) copy-start(bf16[2,256,256]{2,1,0:T(8,128)(2,1)} %param.22) | copy-start | bytes 786436
  34.7 2.4 %copy-start.5 = (s32[2]{0:T(128)S(1)}, s32[2]{0:T(128)}, u32[]{:S(2)}) copy-start(s32[2]{0:T(128)} %param.25) | copy-start | bytes 28
  34.7 2.4 %copy-start.6 = (s32[2]{0:T(128)S(1)}, s32[2]{0:T(128)}, u32[]{:S(2)}) copy-start(s32[2]{0:T(128)} %param.26) | copy-start | bytes 28
  35.8 17.7 %copy-start.1 = (bf16[256,256]{0,1:T(8,128)(2,1)}, bf16[256,256]{0,1:T(8,128)(2,1)S(1)}, u32[]{:S(2)}) copy-start(bf16[256,256]{0,1:T(8,128)(2,1)S(1)} %get-tuple-element.957) | copy-start | bytes 393220
  50.3 4.8 %collective-permute-start.3 = (bf16[1,2,256,256]{3,2,1,0:T(8,128)(2,1)}, bf16[1,2,256,256]{3,2,1,0:T(8,128)(2,1)S(1)}, u32[]{:S(2)}, u32[]{:S(2)}) collective-permute-start(bf16[1,2,256,256]{3,2,1,0:T(8,128)(2,1)} %get-tuple-element.789), channel_id=1, source_target_pairs={{0,512},{1,513},{2,514},{3,515},{4,516},{5,517},{6,518},{7,519},{8... | collective-permute-start | bytes 786440 | tf_op jit(solution)/shard_map/ppermute | solution.py:12
  65.6 20.4 %collective-permute-start.1 = (bf16[1,2,256,256]{3,2,1,0:T(8,128)(2,1)}, bf16[1,2,256,256]{3,2,1,0:T(8,128)(2,1)S(1)}, u32[]{:S(2)}, u32[]{:S(2)}) collective-permute-start(bf16[1,2,256,256]{3,2,1,0:T(8,128)(2,1)} %get-tuple-element.1081), channel_id=1, source_target_pairs={{512,0},{513,1},{514,2},{515,3},{516,4},{517,5},{518,6},{519,7},{5... | collective-permute-start | bytes 786440 | tf_op jit(solution)/shard_map/while/body/eval_jaxpr/ppermute | solution.py:12
  66.8 20.3 %collective-permute-start = (bf16[1,2,256,256]{3,2,1,0:T(8,128)(2,1)S(1)}, bf16[1,2,256,256]{3,2,1,0:T(8,128)(2,1)S(1)}, u32[]{:S(2)}, u32[]{:S(2)}) collective-permute-start(bf16[1,2,256,256]{3,2,1,0:T(8,128)(2,1)S(1)} %get-tuple-element.1077), channel_id=1, source_target_pairs={{0,512},{1,513},{2,514},{3,515},{4,516},{5,517},{6,518},{7,519},{8... | collective-permute-start | bytes 786440 | tf_op jit(solution)/shard_map/while/body/eval_jaxpr/ppermute | solution.py:12
  108.6 11.8 %collective-permute-start.1 = (bf16[1,2,256,256]{3,2,1,0:T(8,128)(2,1)}, bf16[1,2,256,256]{3,2,1,0:T(8,128)(2,1)S(1)}, u32[]{:S(2)}, u32[]{:S(2)}) collective-permute-start(bf16[1,2,256,256]{3,2,1,0:T(8,128)(2,1)} %get-tuple-element.1081), channel_id=1, source_target_pairs={{512,0},{513,1},{514,2},{515,3},{516,4},{517,5},{518,6},{519,7},{5... | collective-permute-start | bytes 786440 | tf_op jit(solution)/shard_map/while/body/eval_jaxpr/ppermute | solution.py:12
  109.9 11.6 %collective-permute-start = (bf16[1,2,256,256]{3,2,1,0:T(8,128)(2,1)S(1)}, bf16[1,2,256,256]{3,2,1,0:T(8,128)(2,1)S(1)}, u32[]{:S(2)}, u32[]{:S(2)}) collective-permute-start(bf16[1,2,256,256]{3,2,1,0:T(8,128)(2,1)S(1)} %get-tuple-element.1077), channel_id=1, source_target_pairs={{0,512},{1,513},{2,514},{3,515},{4,516},{5,517},{6,518},{7,519},{8... | collective-permute-start | bytes 786440 | tf_op jit(solution)/shard_map/while/body/eval_jaxpr/ppermute | solution.py:12
  121.5 1.1 copy-start.2
  141.0 15.3 %collective-permute-start.4 = (bf16[2,1,256,512]{3,2,1,0:T(8,128)(2,1)S(1)}, bf16[2,1,256,512]{3,2,1,0:T(8,128)(2,1)S(1)}, u32[]{:S(2)}, u32[]{:S(2)}) collective-permute-start(bf16[2,1,256,512]{3,2,1,0:T(8,128)(2,1)S(1)} %slice.376), channel_id=1, source_target_pairs={{0,1},{1,2},{2,3},{3,4},{4,5},{5,6},{6,7},{7,8},{8,9},{9,10},{10,1... | collective-permute-start | bytes 1572872 | tf_op jit(solution)/shard_map/ppermute | solution.py:12
where the time goes:
time: 160 us; the launch traced here: 159 us
  starting transfers between devices  56.9 us (36%)
  local copies, waits for them, and re-layouts  27.6 us (17%)
  matrix products  21.2 us (13%)
  loops' own time  20 us (12%)
  other arithmetic  16.4 us (10%)
  waiting for transfers between devices  15.6 us (10%)
    ppermute x7, starting transfers between devices, shifted(): lax.ppermute(value, axis, [(source, source + steps) for source in range(f...  56.9 us
    ppermute x7, waiting for transfers between devices, shifted(): lax.ppermute(value, axis, [(source, source + steps) for source in range(f...  15.6 us
    dynamic_update_slice x2, local copies, waits for them, and re-layouts, backward(): gradient = lax.dynamic_update_slice(gradient, current + patches[0], corner)  13.2 us
    another operation x4, loops' own time, advance(): lax.cond(rear_ok, lambda grad_in: backward(rear_at, arriving[:, 0], arriv...  10.8 us
    another operation x4, loops' own time, advance(): lax.cond(front_ok, lambda saved_in: forward(front_at, start_wave[:, 0], s...  7.8 us
    dot_general x16, matrix products, right_product(): jnp.einsum('bmj,nj->bmn', field, matrix, preferred_element_type=jnp.float32)  5.52 us
    dot_general x16, matrix products, left_product(): jnp.einsum('mj,bjn->bmn', matrix, field, preferred_element_type=jnp.float32)  5.42 us
    another operation x8, other arithmetic, advance(): jnp.stack([factor * leave_re, factor * leave_im], axis=1)  4.3 us
  transfers between devices with their start and end apart: 7, of which 3 were waited for; matrix products, arithmetic and copies ran while one was open for 11% of the time, Pallas kernels for 0%

commit v1 on v0

v1 whole, which is shorter than its diff:
```python
import functools
import math

import jax
import jax.numpy as jnp
import numpy as np
from jax import lax
from jax.experimental import pallas as pl
from jax.experimental.pallas import tpu as pltpu
from jax.sharding import PartitionSpec as P

MESH = pl.DeviceIdType.MESH
F32 = jnp.float32
BF16 = jnp.bfloat16


def dot(a, b):
    return jnp.dot(a, b, preferred_element_type=F32)


def exact_dot(a, b):
    return jnp.dot(a, b, precision=lax.Precision.HIGHEST, preferred_element_type=F32)


def angle_tables(side):
    index = np.arange(side, dtype=np.int64)
    angles = (index[:, None] * index[None, :] % side) * (2.0 * math.pi / side)
    return np.cos(angles).astype(np.float32), np.sin(angles).astype(np.float32)


def kernel(
    tiles,
    side,
    row_ref,
    col_ref,
    count_ref,
    object_hbm,
    probe_hbm,
    turn_hbm,
    measured_hbm,
    cosine_hbm,
    sine_hbm,
    out_ref,
    field,
    probe,
    turn,
    cosine,
    sine,
    measured,
    mine,
    prev,
    send_core,
    send_prev,
    send_next,
    own,
    far,
    kl,
    klt,
    flr,
    flrt,
    flc,
    flct,
    psi0,
    psi1,
    grad,
    grad_core,
    grad_far,
    load_sem,
    scalar_sem,
    core_sem,
    prev_sem,
    next_sem,
    far_sem,
    measured_send,
    measured_sem,
    grad_core_sem,
    grad_send,
    grad_far_sem,
):
    sec = lax.axis_index("sec")
    tile = lax.axis_index("tile")
    other = 1 - sec
    before = lax.rem(tile + tiles - 1, tiles)
    after = lax.rem(tile + 1, tiles)
    half = side // 2

    loads = [
        pltpu.make_async_copy(object_hbm.at[:, 0], field, load_sem.at[0]),
        pltpu.make_async_copy(probe_hbm, probe, load_sem.at[1]),
        pltpu.make_async_copy(turn_hbm, turn, load_sem.at[2]),
        pltpu.make_async_copy(cosine_hbm, cosine, load_sem.at[3]),
        pltpu.make_async_copy(sine_hbm, sine, load_sem.at[4]),
    ]
    for load in loads:
        load.start()

    barrier = pltpu.get_barrier_semaphore()
    partners = [(other, tile), (0, before), (1, before), (0, after), (1, after)]
    for partner in partners:
        pl.semaphore_signal(barrier, inc=1, device_id=partner, device_id_type=MESH)

    line = lax.broadcasted_iota(jnp.int32, (8, side), 0)
    values = jnp.zeros((8, side), jnp.int32)
    for at, value in enumerate((row_ref[0], row_ref[1], col_ref[0], col_ref[1], count_ref[0])):
        values = jnp.where(line == at, value, values)
    mine[...] = values
    pl.semaphore_wait(barrier, len(partners))

    scalars = pltpu.make_async_remote_copy(
        mine, prev, scalar_sem.at[0], scalar_sem.at[1], device_id=(sec, after), device_id_type=MESH
    )
    scalars.start()

    def remote(source, target, send, receive, device):
        return pltpu.make_async_remote_copy(
            source, target, send, receive, device_id=device, device_id_type=MESH
        )

    first = sec == 0
    column = lax.broadcasted_iota(jnp.int32, (side, side), 1)
    row = lax.broadcasted_iota(jnp.int32, (side, side), 0)

    def pick(target, left_col):
        turned = column < left_col
        for part in range(2):
            target[part] = jnp.where(turned, field[part, :, side:], field[part, :, :side])

    loads[0].wait()
    own_vec = (mine[0:1, :], mine[1:2, :], mine[2:3, :], mine[3:4, :], mine[4:5, :])
    pick(send_next, own_vec[3])
    to_next = remote(send_next, far.at[sec], next_sem.at[0], far_sem.at[sec], (1, after))
    to_next.start()
    scalars.wait()
    prev_vec = (prev[0:1, :], prev[1:2, :], prev[2:3, :], prev[3:4, :], prev[4:5, :])
    pick(send_prev, prev_vec[2])
    to_prev = remote(send_prev, far.at[sec], prev_sem.at[0], far_sem.at[sec], (0, before))
    to_prev.start()
    rows_part = pl.ds(pl.multiple_of(sec * half, half), half)
    intensity = remote(
        measured_hbm.at[1, rows_part],
        measured.at[rows_part],
        measured_send.at[0],
        measured_sem.at[sec],
        (1, after),
    )
    intensity.start()
    local_intensity = pltpu.make_async_copy(measured_hbm.at[0], measured, load_sem.at[5])

    @pl.when(first)
    def _():
        local_intensity.start()

    my_row = jnp.where(first, own_vec[0], prev_vec[1])
    my_col = jnp.where(first, own_vec[2], prev_vec[3])
    live = jnp.where(first, (own_vec[4] > 0).astype(F32), (prev_vec[4] > 1).astype(F32))
    their_col = jnp.where(first, prev_vec[3], own_vec[2])
    their_row = jnp.where(first, prev_vec[1], own_vec[0])

    pick(send_core, their_col)
    to_core = remote(send_core, own.at[sec], core_sem.at[0], core_sem.at[1], (other, tile))
    to_core.start()
    pick(own.at[sec], my_col)

    for load in loads[1:]:
        load.wait()
    cos_table = cosine[...]
    sin_table = sine[...]
    phase = turn[...]
    phase_cos = jnp.cos(phase)
    phase_sin = jnp.sin(phase)
    turned_re = cos_table * phase_cos - sin_table * phase_sin
    turned_im = sin_table * phase_cos + cos_table * phase_sin
    scale = 1.0 / side
    k_re = (exact_dot(turned_re, cos_table) + exact_dot(turned_im, sin_table)) * scale
    k_im = (exact_dot(turned_im, cos_table) - exact_dot(turned_re, sin_table)) * scale

    def fill(target, re, im):
        target[:side, :side] = re
        target[:side, side:] = -im
        target[side:, :side] = im
        target[side:, side:] = re

    fill(kl, k_re.astype(BF16), k_im.astype(BF16))
    fill(klt, k_re.T.astype(BF16), -(k_im.T).astype(BF16))

    def one_hot(difference, shift):
        return ((difference & (side - 1)) == (shift & (side - 1))).astype(F32).astype(BF16)

    roll_rows = one_hot(row - column, my_row)
    roll_rows_t = one_hot(column - row, my_row)
    roll_cols = one_hot(row - column, my_col)
    roll_cols_t = one_hot(column - row, my_col)
    norm_scale = 1.0 / math.sqrt(side)
    far_re = (cos_table * norm_scale).astype(BF16)
    far_im = (-sin_table * norm_scale).astype(BF16)
    fill(flr, dot(far_re, roll_rows_t).astype(BF16), dot(far_im, roll_rows_t).astype(BF16))
    fill(flrt, dot(roll_rows, far_re).astype(BF16), -dot(roll_rows, far_im).astype(BF16))
    fill(flc, dot(far_re, roll_cols_t).astype(BF16), dot(far_im, roll_cols_t).astype(BF16))
    fill(flct, dot(roll_cols, far_re).astype(BF16), -dot(roll_cols, far_im).astype(BF16))
    for part in range(2):
        half_way = dot(roll_rows, probe[part]).astype(BF16)
        psi0[part] = dot(half_way, roll_cols_t).astype(BF16)

    in_next = row < my_row
    mine_rows = in_next != first
    in_mine = jnp.where(mine_rows, 1.0, 0.0)
    edge_first = first & (tile == tiles - 1)
    edge_second = jnp.logical_not(first) & (tile == 0)
    own_gate = in_mine * jnp.where(edge_second, 0.0, 1.0)
    far_gate = (1.0 - in_mine) * jnp.where(edge_first, 0.0, 1.0)

    def window(layer):
        return [
            own[layer, part].astype(F32) * own_gate + far[layer, part].astype(F32) * far_gate
            for part in range(2)
        ]

    def wait_recv(target, receive):
        remote(target, target, receive, receive, (other, tile)).wait_recv()

    to_core.wait()
    wait_recv(far.at[0], far_sem.at[0])
    wait_recv(far.at[1], far_sem.at[1])

    def across(value):
        return jnp.concatenate([value[:side], value[side:]], axis=1)

    def down(value):
        return jnp.concatenate([value[:, :side], value[:, side:]], axis=0)

    def transmit(t, w_re, w_im):
        return jnp.concatenate(
            [(t[0] * w_re - t[1] * w_im).astype(BF16), (t[0] * w_im + t[1] * w_re).astype(BF16)],
            axis=1,
        )

    def conj_times(a_re, a_im, b_re, b_im):
        return a_re * b_re + a_im * b_im, a_re * b_im - a_im * b_re

    entered = transmit(window(0), psi0[0].astype(F32), psi0[1].astype(F32))
    inner = dot(entered, klt[...]).astype(BF16)
    psi1[...] = dot(kl[...], down(inner)).astype(BF16)
    window1 = window(1)
    entered = transmit(window1, psi1[:side].astype(F32), psi1[side:].astype(F32))
    inner = dot(entered, flct[...]).astype(BF16)
    leave = dot(flr[...], down(inner)).astype(BF16)

    @pl.when(first)
    def _():
        local_intensity.wait()

    @pl.when(jnp.logical_not(first))
    def _():
        wait_recv(measured.at[:half], measured_sem.at[0])
        wait_recv(measured.at[half:], measured_sem.at[1])

    leave_re = leave[:side].astype(F32)
    leave_im = leave[side:].astype(F32)
    factor = 2.0 * (leave_re * leave_re + leave_im * leave_im - measured[...].astype(F32)) * live
    residual = jnp.concatenate(
        [(factor * leave_re).astype(BF16), (factor * leave_im).astype(BF16)], axis=0
    )

    far_tile = jnp.where(first, after, before)
    inner = dot(flrt[...], residual).astype(BF16)
    spread = dot(across(inner), flc[...]).astype(BF16).astype(F32)
    grad_re, grad_im = conj_times(
        psi1[:side].astype(F32), psi1[side:].astype(F32), spread[:, :side], spread[:, side:]
    )
    grad[1, 0] = grad_re.astype(BF16)
    grad[1, 1] = grad_im.astype(BF16)
    grad_to_far1 = remote(
        grad.at[1], grad_far.at[sec], grad_send.at[1], grad_far_sem.at[sec], (1, far_tile)
    )
    grad_to_far1.start()
    next_re, next_im = conj_times(window1[0], window1[1], spread[:, :side], spread[:, side:])
    entering = jnp.concatenate([next_re.astype(BF16), next_im.astype(BF16)], axis=0)
    inner = dot(klt[...], entering).astype(BF16)
    spread = dot(across(inner), kl[...]).astype(BF16).astype(F32)
    grad_re, grad_im = conj_times(
        psi0[0].astype(F32), psi0[1].astype(F32), spread[:, :side], spread[:, side:]
    )
    grad[0, 0] = grad_re.astype(BF16)
    grad[0, 1] = grad_im.astype(BF16)
    grad_to_far0 = remote(
        grad.at[0], grad_far.at[sec], grad_send.at[0], grad_far_sem.at[sec], (0, far_tile)
    )
    grad_to_far0.start()
    grad_to_core = remote(
        grad.at[other], grad_core, grad_core_sem.at[0], grad_core_sem.at[1], (other, tile)
    )
    grad_to_core.start()

    def put(source, here_rows, left_col, gate, start):
        turned = column < left_col
        for part in range(2):
            value = jnp.where(here_rows, source[part].astype(F32), 0.0) * gate
            left = jnp.where(turned, 0.0, value)
            right = jnp.where(turned, value, 0.0)
            if start:
                out_ref[part, 0, :, :side] = left
                out_ref[part, 0, :, side:] = right
            else:
                out_ref[part, 0, :, :side] += left
                out_ref[part, 0, :, side:] += right

    put(grad.at[sec], mine_rows, my_col, jnp.where(edge_second, 0.0, 1.0), True)
    grad_to_core.wait()
    their_rows = (row < their_row) == first
    put(grad_core, their_rows, their_col, jnp.where(first & (tile == 0), 0.0, 1.0), False)
    wait_recv(grad_far.at[0], grad_far_sem.at[0])
    put(
        grad_far.at[0],
        row < prev_vec[0],
        prev_vec[2],
        jnp.where(tile == 0, 0.0, 1.0),
        False,
    )
    wait_recv(grad_far.at[1], grad_far_sem.at[1])
    put(grad_far.at[1], row >= own_vec[1], own_vec[3], 1.0, False)

    to_next.wait_send()
    to_prev.wait_send()
    intensity.wait_send()
    grad_to_far0.wait_send()
    grad_to_far1.wait_send()


def on_device(tiles, object_field, probe, phases, intensities, pos_row, pos_col, counts):
    side = probe.shape[1]
    cosine, sine = angle_tables(side)
    smem = pl.BlockSpec(memory_space=pltpu.SMEM)
    anywhere = pl.BlockSpec(memory_space=pl.ANY)
    block = (2, side, side)
    wide = (2 * side, 2 * side)
    dma = pltpu.SemaphoreType.DMA
    return pl.pallas_call(
        functools.partial(kernel, tiles, side),
        out_shape=jax.ShapeDtypeStruct(object_field.shape, F32),
        in_specs=[smem] * 3 + [anywhere] * 6,
        out_specs=pl.BlockSpec(memory_space=pltpu.VMEM),
        scratch_shapes=[
            pltpu.VMEM((2, side, object_field.shape[3]), BF16),
            pltpu.VMEM(block, BF16),
            pltpu.VMEM((1, side), F32),
            pltpu.VMEM((side, side), F32),
            pltpu.VMEM((side, side), F32),
            pltpu.VMEM((side, side), BF16),
            pltpu.VMEM((8, side), jnp.int32),
            pltpu.VMEM((8, side), jnp.int32),
            pltpu.VMEM(block, BF16),
            pltpu.VMEM(block, BF16),
            pltpu.VMEM(block, BF16),
            pltpu.VMEM((2,) + block, BF16),
            pltpu.VMEM((2,) + block, BF16),
            pltpu.VMEM(wide, BF16),
            pltpu.VMEM(wide, BF16),
            pltpu.VMEM(wide, BF16),
            pltpu.VMEM(wide, BF16),
            pltpu.VMEM(wide, BF16),
            pltpu.VMEM(wide, BF16),
            pltpu.VMEM(block, BF16),
            pltpu.VMEM((2 * side, side), BF16),
            pltpu.VMEM((2,) + block, BF16),
            pltpu.VMEM(block, BF16),
            pltpu.VMEM((2,) + block, BF16),
            dma((6,)),
            dma((2,)),
            dma((2,)),
            dma((1,)),
            dma((1,)),
            dma((2,)),
            dma((1,)),
            dma((2,)),
            dma((2,)),
            dma((2,)),
            dma((2,)),
        ],
        compiler_params=pltpu.CompilerParams(
            collective_id=0, has_side_effects=True, vmem_limit_bytes=48 * 1024 * 1024
        ),
    )(
        pos_row,
        pos_col,
        counts,
        object_field,
        probe,
        phases.reshape(1, side),
        intensities,
        jnp.asarray(cosine),
        jnp.asarray(sine),
    )


def solution(mesh):
    placed = (
        P(None, "sec", "tile", None),
        P(),
        P(),
        P("tile", None, None),
        P("tile"),
        P("tile"),
        P("tile"),
    )
    return jax.shard_map(
        functools.partial(on_device, mesh.shape["tile"]),
        mesh=mesh,
        in_specs=placed,
        out_specs=P(None, "sec", "tile", None),
        check_vma=False,
    )
```

time: 160 us -> 53.6 us (0.34)
  the two profiles are of different devices: /device:TPU:6 before, /device:TPU:1 now
where the time goes in v1:
time: 53.6 us; the launch traced here: 53.3 us
  Pallas kernels  46.1 us (86%)
  local copies, waits for them, and re-layouts  6.47 us (12%)
  between operations  0.7 us (1%)
    pallas_call x1, Pallas kernels, on_device(): pl.pallas_call(functools.partial(kernel, tiles, side), out_shape=jax.Shap...  46.1 us
    unnamed x17, local copies, waits for them, and re-layouts  6.47 us

profile of v1, /device:TPU:1, one launch (start us, length us, event | category | flops | bytes accessed | tf_op | source)
XLA Modules:
  0.0 53.3 jit_solution(2224036493284559688)
XLA Ops:
  0.0 0.0 copy-start.7
  0.7 0.0 copy-start.5
  0.7 0.0 copy-start.6
  0.7 0.0 copy-done.7
  0.7 0.7 %copy-done.5 = f32[256]{0:T(256)S(1)} copy-done((f32[256]{0:T(256)S(1)}, f32[256]{0:T(256)}, u32[]{:S(2)}) %copy-start.5) | copy-done | bytes 1048
  1.3 0.0 copy-done.6
  1.4 0.0 copy-start
  1.4 1.0 %copy-done = bf16[2,1,256,512]{3,2,1,0:T(8,128)(2,1)S(1)} copy-done((bf16[2,1,256,512]{3,2,1,0:T(8,128)(2,1)S(1)}, bf16[2,1,256,512]{3,2,1,0:T(8,128)(2,1)}, u32[]{:S(2)}) %copy-start) | copy-done | bytes 524312
  2.4 0.0 copy-start.1
  2.4 0.9 %copy-done.1 = bf16[2,256,256]{2,1,0:T(8,128)(2,1)S(1)} copy-done((bf16[2,256,256]{2,1,0:T(8,128)(2,1)S(1)}, bf16[2,256,256]{2,1,0:T(8,128)(2,1)}, u32[]{:S(2)}) %copy-start.1) | copy-done | bytes 262168
  3.3 0.0 copy-start.2
  3.3 0.9 %copy-done.2 = bf16[2,256,256]{2,1,0:T(8,128)(2,1)S(1)} copy-done((bf16[2,256,256]{2,1,0:T(8,128)(2,1)S(1)}, bf16[2,256,256]{2,1,0:T(8,128)(2,1)}, u32[]{:S(2)}) %copy-start.2) | copy-done | bytes 262168
  4.3 0.0 copy-start.3
  4.3 0.9 %copy-done.3 = f32[256,256]{1,0:T(8,128)S(1)} copy-done((f32[256,256]{1,0:T(8,128)S(1)}, f32[256,256]{1,0:T(8,128)}, u32[]{:S(2)}) %copy-start.3) | copy-done | bytes 262168
  5.2 0.0 copy-start.4
  5.2 0.9 %copy-done.4 = f32[256,256]{1,0:T(8,128)S(1)} copy-done((f32[256,256]{1,0:T(8,128)S(1)}, f32[256,256]{1,0:T(8,128)}, u32[]{:S(2)}) %copy-start.4) | copy-done | bytes 262168
  6.2 46.1 %shard_map.91 = f32[2,1,256,512]{3,2,1,0:T(8,128)S(1)} custom-call(s32[2]{0:T(128)S(1)} %copy-done.6, s32[2]{0:T(128)S(1)} %copy-done.7, s32[1]{0:T(128)S(6)} %copy.11.count_ref, bf16[2,1,256,512]{3,2,1,0:T(8,128)(2,1)S(1)} %copy-done, bf16[2,256,256]{2,1,0:T(8,128)(2,1)S(1)} %copy-done.1, f32[1,256]{1,0:T(1,128)S(1)} %bitcast.1, ...), custom_call_target="tpu_custom_call" | custom-call | tf_op jit(solution)/shard_map/pallas_call | solution.py:337
  52.3 1.0 %copy.12 = f32[2,1,256,512]{3,2,1,0:T(8,128)} copy(f32[2,1,256,512]{3,2,1,0:T(8,128)S(1)} %shard_map.91) | data formatting | bytes 2097152
Async XLA Ops:
  0.0 0.7 %copy-start.7 = (s32[2]{0:T(128)S(1)}, s32[2]{0:T(128)}, u32[]{:S(2)}) copy-start(s32[2]{0:T(128)} %col_ref.1) | copy-start | bytes 28
  0.7 0.7 %copy-start.5 = (f32[256]{0:T(256)S(1)}, f32[256]{0:T(256)}, u32[]{:S(2)}) copy-start(f32[256]{0:T(256)} %param.11) | copy-start | bytes 3076
  0.7 0.7 %copy-start.6 = (s32[2]{0:T(128)S(1)}, s32[2]{0:T(128)}, u32[]{:S(2)}) copy-start(s32[2]{0:T(128)} %row_ref.1) | copy-start | bytes 28
  1.4 1.0 %copy-start = (bf16[2,1,256,512]{3,2,1,0:T(8,128)(2,1)S(1)}, bf16[2,1,256,512]{3,2,1,0:T(8,128)(2,1)}, u32[]{:S(2)}) copy-start(bf16[2,1,256,512]{3,2,1,0:T(8,128)(2,1)} %object_hbm.1) | copy-start | bytes 1572868
  2.4 0.9 %copy-start.1 = (bf16[2,256,256]{2,1,0:T(8,128)(2,1)S(1)}, bf16[2,256,256]{2,1,0:T(8,128)(2,1)}, u32[]{:S(2)}) copy-start(bf16[2,256,256]{2,1,0:T(8,128)(2,1)} %probe_hbm.1) | copy-start | bytes 786436
  3.3 0.9 %copy-start.2 = (bf16[2,256,256]{2,1,0:T(8,128)(2,1)S(1)}, bf16[2,256,256]{2,1,0:T(8,128)(2,1)}, u32[]{:S(2)}) copy-start(bf16[2,256,256]{2,1,0:T(8,128)(2,1)} %measured_hbm.1) | copy-start | bytes 786436
  4.3 0.9 %copy-start.3 = (f32[256,256]{1,0:T(8,128)S(1)}, f32[256,256]{1,0:T(8,128)}, u32[]{:S(2)}) copy-start(f32[256,256]{1,0:T(8,128)} %constant.5.clone.sine_hbm) | copy-start | bytes 786436
  5.2 0.9 %copy-start.4 = (f32[256,256]{1,0:T(8,128)S(1)}, f32[256,256]{1,0:T(8,128)}, u32[]{:S(2)}) copy-start(f32[256,256]{1,0:T(8,128)} %constant.4.clone.cosine_hbm) | copy-start | bytes 786436

commit v2 on v1

--- a/solution.py
+++ b/solution.py
@@ -31,9 +31,9 @@
 def kernel(
     tiles,
     side,
-    row_ref,
-    col_ref,
     count_ref,
+    row_hbm,
+    col_hbm,
     object_hbm,
     probe_hbm,
     turn_hbm,
@@ -41,6 +41,8 @@
     cosine_hbm,
     sine_hbm,
     out_ref,
+    row_ref,
+    col_ref,
     field,
     probe,
     turn,
@@ -50,7 +52,6 @@
     mine,
     prev,
     send_core,
-    send_prev,
     send_next,
     own,
     far,
@@ -68,10 +69,8 @@
     load_sem,
     scalar_sem,
     core_sem,
-    prev_sem,
     next_sem,
     far_sem,
-    measured_send,
     measured_sem,
     grad_core_sem,
     grad_send,
@@ -82,34 +81,31 @@
     other = 1 - sec
     before = lax.rem(tile + tiles - 1, tiles)
     after = lax.rem(tile + 1, tiles)
-    half = side // 2
 
     loads = [
-        pltpu.make_async_copy(object_hbm.at[:, 0], field, load_sem.at[0]),
-        pltpu.make_async_copy(probe_hbm, probe, load_sem.at[1]),
-        pltpu.make_async_copy(turn_hbm, turn, load_sem.at[2]),
-        pltpu.make_async_copy(cosine_hbm, cosine, load_sem.at[3]),
-        pltpu.make_async_copy(sine_hbm, sine, load_sem.at[4]),
+        pltpu.make_async_copy(row_hbm, row_ref, load_sem.at[0]),
+        pltpu.make_async_copy(col_hbm, col_ref, load_sem.at[1]),
+        pltpu.make_async_copy(object_hbm.at[:, 0], field, load_sem.at[2]),
+        pltpu.make_async_copy(probe_hbm, probe, load_sem.at[3]),
+        pltpu.make_async_copy(turn_hbm, turn, load_sem.at[4]),
+        pltpu.make_async_copy(cosine_hbm, cosine, load_sem.at[5]),
+        pltpu.make_async_copy(sine_hbm, sine, load_sem.at[6]),
     ]
     for load in loads:
         load.start()
 
     barrier = pltpu.get_barrier_semaphore()
-    partners = [(other, tile), (0, before), (1, before), (0, after), (1, after)]
+    partners = [(other, tile), (0, before), (1, before)]
     for partner in partners:
         pl.semaphore_signal(barrier, inc=1, device_id=partner, device_id_type=MESH)
 
+    for load in loads[:2]:
+        load.wait()
     line = lax.broadcasted_iota(jnp.int32, (8, side), 0)
     values = jnp.zeros((8, side), jnp.int32)
     for at, value in enumerate((row_ref[0], row_ref[1], col_ref[0], col_ref[1], count_ref[0])):
         values = jnp.where(line == at, value, values)
     mine[...] = values
-    pl.semaphore_wait(barrier, len(partners))
-
-    scalars = pltpu.make_async_remote_copy(
-        mine, prev, scalar_sem.at[0], scalar_sem.at[1], device_id=(sec, after), device_id_type=MESH
-    )
-    scalars.start()
 
     def remote(source, target, send, receive, device):
         return pltpu.make_async_remote_copy(
@@ -125,43 +121,35 @@
         for part in range(2):
             target[part] = jnp.where(turned, field[part, :, side:], field[part, :, :side])
 
-    loads[0].wait()
-    own_vec = (mine[0:1, :], mine[1:2, :], mine[2:3, :], mine[3:4, :], mine[4:5, :])
-    pick(send_next, own_vec[3])
-    to_next = remote(send_next, far.at[sec], next_sem.at[0], far_sem.at[sec], (1, after))
-    to_next.start()
+    loads[2].wait()
+    pick(send_next.at[0], col_ref[0])
+    pl.semaphore_wait(barrier, len(partners))
+    to_next = [
+        remote(send_next.at[slot], far.at[sec], next_sem.at[slot], far_sem.at[sec], (slot, after))
+        for slot in range(2)
+    ]
+    to_next[0].start()
+    scalars = remote(mine, prev, scalar_sem.at[0], scalar_sem.at[1], (sec, after))
+    scalars.start()
+    pick(send_next.at[1], col_ref[1])
+    to_next[1].start()
+    intensity = remote(
+        measured_hbm.at[sec], measured, measured_sem.at[0], measured_sem.at[1], (sec, after)
+    )
+    intensity.start()
+
     scalars.wait()
-    prev_vec = (prev[0:1, :], prev[1:2, :], prev[2:3, :], prev[3:4, :], prev[4:5, :])
-    pick(send_prev, prev_vec[2])
-    to_prev = remote(send_prev, far.at[sec], prev_sem.at[0], far_sem.at[sec], (0, before))
-    to_prev.start()
-    rows_part = pl.ds(pl.multiple_of(sec * half, half), half)
-    intensity = remote(
-        measured_hbm.at[1, rows_part],
-        measured.at[rows_part],
-        measured_send.at[0],
-        measured_sem.at[sec],
-        (1, after),
-    )
-    intensity.start()
-    local_intensity = pltpu.make_async_copy(measured_hbm.at[0], measured, load_sem.at[5])
-
-    @pl.when(first)
-    def _():
-        local_intensity.start()
-
-    my_row = jnp.where(first, own_vec[0], prev_vec[1])
-    my_col = jnp.where(first, own_vec[2], prev_vec[3])
-    live = jnp.where(first, (own_vec[4] > 0).astype(F32), (prev_vec[4] > 1).astype(F32))
-    their_col = jnp.where(first, prev_vec[3], own_vec[2])
-    their_row = jnp.where(first, prev_vec[1], own_vec[0])
-
+    my_row = jnp.where(first, prev[0:1, :], prev[1:2, :])
+    my_col = jnp.where(first, prev[2:3, :], prev[3:4, :])
+    their_row = jnp.where(first, prev[1:2, :], prev[0:1, :])
+    their_col = jnp.where(first, prev[3:4, :], prev[2:3, :])
+    live = (prev[4:5, :] > sec).astype(F32)
     pick(send_core, their_col)
     to_core = remote(send_core, own.at[sec], core_sem.at[0], core_sem.at[1], (other, tile))
     to_core.start()
     pick(own.at[sec], my_col)
 
-    for load in loads[1:]:
+    for load in loads[3:]:
         load.wait()
     cos_table = cosine[...]
     sin_table = sine[...]
@@ -202,12 +190,9 @@
         psi0[part] = dot(half_way, roll_cols_t).astype(BF16)
 
     in_next = row < my_row
-    mine_rows = in_next != first
-    in_mine = jnp.where(mine_rows, 1.0, 0.0)
-    edge_first = first & (tile == tiles - 1)
-    edge_second = jnp.logical_not(first) & (tile == 0)
-    own_gate = in_mine * jnp.where(edge_second, 0.0, 1.0)
-    far_gate = (1.0 - in_mine) * jnp.where(edge_first, 0.0, 1.0)
+    has_next = jnp.where(tile == 0, 0.0, 1.0)
+    own_gate = jnp.where(in_next, has_next, 0.0)
+    far_gate = jnp.where(in_next, 0.0, 1.0)
 
     def window(layer):
         return [
@@ -245,15 +230,7 @@
     inner = dot(entered, flct[...]).astype(BF16)
     leave = dot(flr[...], down(inner)).astype(BF16)
 
-    @pl.when(first)
-    def _():
-        local_intensity.wait()
-
-    @pl.when(jnp.logical_not(first))
-    def _():
-        wait_recv(measured.at[:half], measured_sem.at[0])
-        wait_recv(measured.at[half:], measured_sem.at[1])
-
+    intensity.wait_recv()
     leave_re = leave[:side].astype(F32)
     leave_im = leave[side:].astype(F32)
     factor = 2.0 * (leave_re * leave_re + leave_im * leave_im - measured[...].astype(F32)) * live
@@ -261,7 +238,6 @@
         [(factor * leave_re).astype(BF16), (factor * leave_im).astype(BF16)], axis=0
     )
 
-    far_tile = jnp.where(first, after, before)
     inner = dot(flrt[...], residual).astype(BF16)
     spread = dot(across(inner), flc[...]).astype(BF16).astype(F32)
     grad_re, grad_im = conj_times(
@@ -270,7 +246,7 @@
     grad[1, 0] = grad_re.astype(BF16)
     grad[1, 1] = grad_im.astype(BF16)
     grad_to_far1 = remote(
-        grad.at[1], grad_far.at[sec], grad_send.at[1], grad_far_sem.at[sec], (1, far_tile)
+        grad.at[1], grad_far.at[sec], grad_send.at[1], grad_far_sem.at[sec], (1, before)
     )
     grad_to_far1.start()
     next_re, next_im = conj_times(window1[0], window1[1], spread[:, :side], spread[:, side:])
@@ -283,7 +259,7 @@
     grad[0, 0] = grad_re.astype(BF16)
     grad[0, 1] = grad_im.astype(BF16)
     grad_to_far0 = remote(
-        grad.at[0], grad_far.at[sec], grad_send.at[0], grad_far_sem.at[sec], (0, far_tile)
+        grad.at[0], grad_far.at[sec], grad_send.at[0], grad_far_sem.at[sec], (0, before)
     )
     grad_to_far0.start()
     grad_to_core = remote(
@@ -304,23 +280,15 @@
                 out_ref[part, 0, :, :side] += left
                 out_ref[part, 0, :, side:] += right
 
-    put(grad.at[sec], mine_rows, my_col, jnp.where(edge_second, 0.0, 1.0), True)
+    put(grad.at[sec], in_next, my_col, has_next, True)
+    for slot in range(2):
+        wait_recv(grad_far.at[slot], grad_far_sem.at[slot])
+        put(grad_far.at[slot], row >= row_ref[slot], col_ref[slot], 1.0, False)
     grad_to_core.wait()
-    their_rows = (row < their_row) == first
-    put(grad_core, their_rows, their_col, jnp.where(first & (tile == 0), 0.0, 1.0), False)
-    wait_recv(grad_far.at[0], grad_far_sem.at[0])
-    put(
-        grad_far.at[0],
-        row < prev_vec[0],
-        prev_vec[2],
-        jnp.where(tile == 0, 0.0, 1.0),
-        False,
-    )
-    wait_recv(grad_far.at[1], grad_far_sem.at[1])
-    put(grad_far.at[1], row >= own_vec[1], own_vec[3], 1.0, False)
-
-    to_next.wait_send()
-    to_prev.wait_send()
+    put(grad_core, row < their_row, their_col, has_next, False)
+
+    for sent in to_next:
+        sent.wait_send()
     intensity.wait_send()
     grad_to_far0.wait_send()
     grad_to_far1.wait_send()
@@ -329,17 +297,18 @@
 def on_device(tiles, object_field, probe, phases, intensities, pos_row, pos_col, counts):
     side = probe.shape[1]
     cosine, sine = angle_tables(side)
-    smem = pl.BlockSpec(memory_space=pltpu.SMEM)
-    anywhere = pl.BlockSpec(memory_space=pl.ANY)
+    anywhere = pl.BlockSpec(memory_space=pltpu.HBM)
     block = (2, side, side)
     wide = (2 * side, 2 * side)
     dma = pltpu.SemaphoreType.DMA
     return pl.pallas_call(
         functools.partial(kernel, tiles, side),
         out_shape=jax.ShapeDtypeStruct(object_field.shape, F32),
-        in_specs=[smem] * 3 + [anywhere] * 6,
+        in_specs=[pl.BlockSpec(memory_space=pltpu.SMEM)] + [anywhere] * 8,
         out_specs=pl.BlockSpec(memory_space=pltpu.VMEM),
         scratch_shapes=[
+            pltpu.SMEM((2,), jnp.int32),
+            pltpu.SMEM((2,), jnp.int32),
             pltpu.VMEM((2, side, object_field.shape[3]), BF16),
             pltpu.VMEM(block, BF16),
             pltpu.VMEM((1, side), F32),
@@ -349,8 +318,7 @@
             pltpu.VMEM((8, side), jnp.int32),
             pltpu.VMEM((8, side), jnp.int32),
             pltpu.VMEM(block, BF16),
-            pltpu.VMEM(block, BF16),
-            pltpu.VMEM(block, BF16),
+            pltpu.VMEM((2,) + block, BF16),
             pltpu.VMEM((2,) + block, BF16),
             pltpu.VMEM((2,) + block, BF16),
             pltpu.VMEM(wide, BF16),
@@ -364,13 +332,11 @@
             pltpu.VMEM((2,) + block, BF16),
             pltpu.VMEM(block, BF16),
             pltpu.VMEM((2,) + block, BF16),
-            dma((6,)),
-            dma((2,)),
-            dma((2,)),
-            dma((1,)),
-            dma((1,)),
-            dma((2,)),
-            dma((1,)),
+            dma((7,)),
+            dma((2,)),
+            dma((2,)),
+            dma((2,)),
+            dma((2,)),
             dma((2,)),
             dma((2,)),
             dma((2,)),
@@ -380,15 +346,20 @@
             collective_id=0, has_side_effects=True, vmem_limit_bytes=48 * 1024 * 1024
         ),
     )(
-        pos_row,
-        pos_col,
         counts,
-        object_field,
-        probe,
-        phases.reshape(1, side),
-        intensities,
-        jnp.asarray(cosine),
-        jnp.asarray(sine),
+        *(
+            pltpu.with_memory_space_constraint(value, pltpu.HBM)
+            for value in (
+                pos_row,
+                pos_col,
+                object_field,
+                probe,
+                phases.reshape(1, side),
+                intensities,
+                jnp.asarray(cosine),
+                jnp.asarray(sine),
+            )
+        )
     )
 
 

time: 53.6 us -> 51.9 us (0.968)
  local copies, waits for them, and re-layouts: 6.47 us -> 0.97 us
  Pallas kernels: 46.1 us -> 50.1 us
    unnamed x17 -> x1, local copies, waits for them, and re-layouts: 6.47 us -> 0.97 us
    pallas_call x1, Pallas kernels: 46.1 us -> 50.1 us  [on_device(): pl.pallas_call(functools.partial(kernel, tiles, side), out_shape=jax.Shap...]
where the time goes in v2:
time: 51.9 us; the launch traced here: 51.7 us
  Pallas kernels  50.1 us (97%)
  local copies, waits for them, and re-layouts  0.97 us (2%)
  between operations  0.66 us (1%)
    pallas_call x1, Pallas kernels, on_device(): pl.pallas_call(functools.partial(kernel, tiles, side), out_shape=jax.Shap...  50.1 us

profile of v2, /device:TPU:1, one launch (start us, length us, event | category | flops | bytes accessed | tf_op | source)
XLA Modules:
  0.0 51.7 jit_solution(18121188842681463689)
XLA Ops:
  0.7 50.1 %shard_map.91 = f32[2,1,256,512]{3,2,1,0:T(8,128)S(1)} custom-call(s32[1]{0:T(128)S(6)} %copy.11.count_ref, s32[2]{0:T(128)} %row_hbm.1, s32[2]{0:T(128)} %col_hbm.1, bf16[2,1,256,512]{3,2,1,0:T(8,128)(2,1)} %object_hbm.1, bf16[2,256,256]{2,1,0:T(8,128)(2,1)} %probe_hbm.1, f32[1,256]{1,0:T(1,128)} %bitcast.1, bf16[2,256,256]{2,1,0:T(8,128)(2,1)} %measured_hbm.1, ...), custom_call_target="tpu_custom_call" | custom-call | tf_op jit(solution)/shard_map/pallas_call | solution.py:304
  50.8 1.0 %copy.12 = f32[2,1,256,512]{3,2,1,0:T(8,128)} copy(f32[2,1,256,512]{3,2,1,0:T(8,128)S(1)} %shard_map.91) | data formatting | bytes 2097152

commit v3 on v2

v3 whole, which is shorter than its diff:
```python
import functools
import math

import jax
import jax.numpy as jnp
import numpy as np
from jax import lax
from jax.experimental import pallas as pl
from jax.experimental.pallas import tpu as pltpu
from jax.sharding import PartitionSpec as P

MESH = pl.DeviceIdType.MESH
F32 = jnp.float32
BF16 = jnp.bfloat16


def dot(a, b):
    return jnp.dot(a, b, preferred_element_type=F32)


def exact_dot(a, b):
    return jnp.dot(a, b, precision=lax.Precision.HIGHEST, preferred_element_type=F32)


def angle_tables(side):
    index = np.arange(side, dtype=np.int64)
    angles = (index[:, None] * index[None, :] % side) * (2.0 * math.pi / side)
    return np.cos(angles).astype(np.float32), np.sin(angles).astype(np.float32)


def kernel(
    tiles,
    side,
    count_ref,
    row_hbm,
    col_hbm,
    object_hbm,
    probe_hbm,
    turn_hbm,
    measured_hbm,
    cosine_hbm,
    sine_hbm,
    out_ref,
    row_ref,
    col_ref,
    field,
    probe,
    turn,
    cosine,
    sine,
    measured,
    mine,
    prev,
    up,
    down,
    core_up,
    core_down,
    far_up,
    far_down,
    kl,
    klt,
    flr,
    flrt,
    flc,
    flct,
    psi0,
    psi1,
    grad,
    grad_core,
    load_sem,
    ready_sem,
    scalar_sem,
    core_send,
    core_sem,
    up_send,
    down_send,
    far_up_sem,
    far_down_sem,
    measured_sem,
    grad_send,
    grad_sem,
):
    sec = lax.axis_index("sec")
    tile = lax.axis_index("tile")
    other = 1 - sec
    first = sec == 0
    has_prev = tile > 0
    has_next = tile < tiles - 1
    before = lax.rem(tile + tiles - 1, tiles)
    after = lax.rem(tile + 1, tiles)

    loads = [
        pltpu.make_async_copy(row_hbm, row_ref, load_sem.at[0]),
        pltpu.make_async_copy(col_hbm, col_ref, load_sem.at[1]),
        pltpu.make_async_copy(object_hbm.at[:, 0], field, load_sem.at[2]),
        pltpu.make_async_copy(measured_hbm.at[sec], measured.at[0], load_sem.at[3]),
        pltpu.make_async_copy(probe_hbm, probe, load_sem.at[4]),
        pltpu.make_async_copy(turn_hbm, turn, load_sem.at[5]),
        pltpu.make_async_copy(cosine_hbm, cosine, load_sem.at[6]),
        pltpu.make_async_copy(sine_hbm, sine, load_sem.at[7]),
    ]
    for load in loads:
        load.start()

    def signal(semaphore, device):
        pl.semaphore_signal(semaphore, inc=1, device_id=device, device_id_type=MESH)

    def remote(source, target, send, receive, device):
        return pltpu.make_async_remote_copy(
            source, target, send, receive, device_id=device, device_id_type=MESH
        )

    barrier = pltpu.get_barrier_semaphore()
    signal(barrier, (other, tile))

    @pl.when(has_prev)
    def _():
        signal(barrier, (0, before))
        signal(barrier, (1, before))

    @pl.when(jnp.logical_not(has_prev))
    def _():
        prev[...] = jnp.zeros_like(prev)
        far_up[...] = jnp.zeros_like(far_up)
        measured[1] = jnp.zeros_like(measured[1])

    @pl.when(jnp.logical_not(has_next))
    def _():
        far_down[...] = jnp.zeros_like(far_down)

    for load in loads[:2]:
        load.wait()
    line = lax.broadcasted_iota(jnp.int32, (8, side), 0)
    values = jnp.zeros((8, side), jnp.int32)
    for at, value in enumerate((row_ref[0], row_ref[1], col_ref[0], col_ref[1], count_ref[0])):
        values = jnp.where(line == at, value, values)
    mine[...] = values

    column = lax.broadcasted_iota(jnp.int32, (side, side), 1)
    row = lax.broadcasted_iota(jnp.int32, (side, side), 0)

    def pick(target, left_col):
        turned = column < left_col
        for part in range(2):
            target[part] = jnp.where(turned, field[part, :, side:], field[part, :, :side])

    to_up = [
        remote(up.at[slot], far_up.at[sec], up_send.at[slot], far_up_sem.at[sec], (slot, after))
        for slot in range(2)
    ]
    scalars = remote(mine, prev, scalar_sem.at[0], scalar_sem.at[1], (sec, after))
    intensity = remote(
        measured_hbm.at[sec], measured.at[1], measured_sem.at[0], measured_sem.at[1], (sec, after)
    )
    loads[2].wait()
    pick(up.at[0], col_ref[0])
    pl.semaphore_wait(barrier, jnp.where(has_next, 3, 1))

    @pl.when(has_next)
    def _():
        to_up[0].start()
        scalars.start()
        signal(ready_sem, (other, after))

    pick(up.at[1], col_ref[1])

    @pl.when(has_next)
    def _():
        to_up[1].start()
        intensity.start()

    to_core_up = remote(
        up.at[other], core_up, core_send.at[0], core_sem.at[0], (other, tile)
    )
    to_core_up.start()

    to_down = [
        remote(
            down.at[slot], far_down.at[sec], down_send.at[slot], far_down_sem.at[sec], (slot, before)
        )
        for slot in range(2)
    ]

    @pl.when(has_prev)
    def _():
        scalars.wait_recv()
        pl.semaphore_wait(ready_sem, 1)

    for slot in range(2):
        pick(down.at[slot], prev[2 + slot : 3 + slot, :])

        @pl.when(has_prev)
        def _():
            to_down[slot].start()

    to_core_down = remote(
        down.at[other], core_down, core_send.at[1], core_sem.at[1], (other, tile)
    )
    to_core_down.start()

    def places(values):
        rows = (values[0:1, :], values[1:2, :])
        cols = (values[2:3, :], values[3:4, :])
        live = (values[4:5, :] > sec).astype(F32)
        my = (jnp.where(first, rows[0], rows[1]), jnp.where(first, cols[0], cols[1]))
        their = (jnp.where(first, rows[1], rows[0]), jnp.where(first, cols[1], cols[0]))
        return my, their, live

    here = places(mine)
    there = places(prev)

    for load in loads[3:]:
        load.wait()
    cos_table = cosine[...]
    sin_table = sine[...]
    phase = turn[...]
    phase_cos = jnp.cos(phase)
    phase_sin = jnp.sin(phase)
    turned_re = cos_table * phase_cos - sin_table * phase_sin
    turned_im = sin_table * phase_cos + cos_table * phase_sin
    scale = 1.0 / side
    k_re = (exact_dot(turned_re, cos_table) + exact_dot(turned_im, sin_table)) * scale
    k_im = (exact_dot(turned_im, cos_table) - exact_dot(turned_re, sin_table)) * scale

    def fill(target, re, im):
        target[:side, :side] = re
        target[:side, side:] = -im
        target[side:, :side] = im
        target[side:, side:] = re

    fill(kl, k_re.astype(BF16), k_im.astype(BF16))
    fill(klt, k_re.T.astype(BF16), -(k_im.T).astype(BF16))

    def one_hot(difference, shift):
        return ((difference & (side - 1)) == (shift & (side - 1))).astype(F32).astype(BF16)

    norm_scale = 1.0 / math.sqrt(side)
    far_re = (cos_table * norm_scale).astype(BF16)
    far_im = (-sin_table * norm_scale).astype(BF16)
    for at, (my_row, my_col) in enumerate((here[0], there[0])):
        roll_rows = one_hot(row - column, my_row)
        roll_rows_t = one_hot(column - row, my_row)
        roll_cols = one_hot(row - column, my_col)
        roll_cols_t = one_hot(column - row, my_col)
        fill(flr.at[at], dot(far_re, roll_rows_t).astype(BF16), dot(far_im, roll_rows_t).astype(BF16))
        fill(flrt.at[at], dot(roll_rows, far_re).astype(BF16), -dot(roll_rows, far_im).astype(BF16))
        fill(flc.at[at], dot(far_re, roll_cols_t).astype(BF16), dot(far_im, roll_cols_t).astype(BF16))
        fill(flct.at[at], dot(roll_cols, far_re).astype(BF16), -dot(roll_cols, far_im).astype(BF16))
        for part in range(2):
            half_way = dot(roll_rows, probe[part]).astype(BF16)
            psi0[at, part] = dot(half_way, roll_cols_t).astype(BF16)

    def wait_recv(target, receive):
        remote(target, target, receive, receive, (other, tile)).wait_recv()

    def across(value):
        return jnp.concatenate([value[:side], value[side:]], axis=1)

    def stacked(value):
        return jnp.concatenate([value[:, :side], value[:, side:]], axis=0)

    def transmit(t, w_re, w_im):
        return jnp.concatenate(
            [(t[0] * w_re - t[1] * w_im).astype(BF16), (t[0] * w_im + t[1] * w_re).astype(BF16)],
            axis=1,
        )

    def conj_times(a_re, a_im, b_re, b_im):
        return a_re * b_re + a_im * b_im, a_re * b_im - a_im * b_re

    def run(at, my_row, live, window, wait_measured):
        in_next = row < my_row
        w_re, w_im = psi0[at, 0].astype(F32), psi0[at, 1].astype(F32)
        entered = transmit(window(0, in_next), w_re, w_im)
        inner = dot(entered, klt[...]).astype(BF16)
        psi1[...] = dot(kl[...], stacked(inner)).astype(BF16)
        window1 = window(1, in_next)
        entered = transmit(window1, psi1[:side].astype(F32), psi1[side:].astype(F32))
        inner = dot(entered, flct[at]).astype(BF16)
        leave = dot(flr[at], stacked(inner)).astype(BF16)
        wait_measured()
        leave_re = leave[:side].astype(F32)
        leave_im = leave[side:].astype(F32)
        level = measured[at].astype(F32)
        factor = 2.0 * (leave_re * leave_re + leave_im * leave_im - level) * live
        residual = jnp.concatenate(
            [(factor * leave_re).astype(BF16), (factor * leave_im).astype(BF16)], axis=0
        )
        inner = dot(flrt[at], residual).astype(BF16)
        spread = dot(across(inner), flc[at]).astype(BF16).astype(F32)
        s_re, s_im = spread[:, :side], spread[:, side:]
        grad_re, grad_im = conj_times(
            psi1[:side].astype(F32), psi1[side:].astype(F32), s_re, s_im
        )
        grad[at, 1, 0] = grad_re.astype(BF16)
        grad[at, 1, 1] = grad_im.astype(BF16)
        next_re, next_im = conj_times(window1[0], window1[1], s_re, s_im)
        entering = jnp.concatenate([next_re.astype(BF16), next_im.astype(BF16)], axis=0)
        inner = dot(klt[...], entering).astype(BF16)
        spread = dot(across(inner), kl[...]).astype(BF16).astype(F32)
        grad_re, grad_im = conj_times(w_re, w_im, spread[:, :side], spread[:, side:])
        grad[at, 0, 0] = grad_re.astype(BF16)
        grad[at, 0, 1] = grad_im.astype(BF16)

    def mixed(in_next, next_block, home_block):
        return [
            jnp.where(in_next, next_block[part].astype(F32), home_block[part].astype(F32))
            for part in range(2)
        ]

    def choose(layer, local, received):
        is_local = sec == layer
        return [
            jnp.where(is_local, local[part].astype(F32), received[part].astype(F32))
            for part in range(2)
        ]

    def put(source, here_rows, left_col, start=False):
        turned = column < left_col
        for part in range(2):
            value = jnp.where(here_rows, source[part].astype(F32), 0.0)
            left = jnp.where(turned, 0.0, value)
            right = jnp.where(turned, value, 0.0)
            if start:
                out_ref[part, 0, :, :side] = left
                out_ref[part, 0, :, side:] = right
            else:
                out_ref[part, 0, :, :side] += left
                out_ref[part, 0, :, side:] += right

    to_core_grad = [
        remote(
            grad.at[at, other], grad_core.at[at], grad_send.at[at], grad_sem.at[at], (other, tile)
        )
        for at in range(2)
    ]

    wait_recv(core_up, core_sem.at[0])

    @pl.when(has_next)
    def _():
        wait_recv(far_down.at[0], far_down_sem.at[0])
        wait_recv(far_down.at[1], far_down_sem.at[1])

    (my_row, my_col), (their_row, their_col), live = here
    run(
        0,
        my_row,
        live,
        lambda layer, in_next: mixed(
            in_next, far_down[layer], choose(layer, up[sec], core_up[...])
        ),
        lambda: None,
    )
    to_core_grad[0].start()
    put(grad[0, sec], row >= my_row, my_col, True)

    (prev_row, prev_col), (prev_their_row, prev_their_col), live = there
    wait_recv(core_down, core_sem.at[1])

    @pl.when(has_prev)
    def _():
        wait_recv(far_up.at[0], far_up_sem.at[0])
        wait_recv(far_up.at[1], far_up_sem.at[1])

    def wait_measured():
        @pl.when(has_prev)
        def _():
            intensity.wait_recv()

    run(
        1,
        prev_row,
        live,
        lambda layer, in_next: mixed(
            in_next, choose(layer, down[sec], core_down[...]), far_up[layer]
        ),
        wait_measured,
    )
    to_core_grad[1].start()
    to_core_grad[0].wait_recv()
    put(grad_core[0], row >= their_row, their_col)
    put(grad[1, sec], (row < prev_row) & has_prev, prev_col)
    to_core_grad[1].wait_recv()
    put(grad_core[1], (row < prev_their_row) & has_prev, prev_their_col)

    for sent in (to_core_up, to_core_down, to_core_grad[0], to_core_grad[1]):
        sent.wait_send()

    @pl.when(has_next)
    def _():
        for sent in (to_up[0], to_up[1], scalars, intensity):
            sent.wait_send()

    @pl.when(has_prev)
    def _():
        to_down[0].wait_send()
        to_down[1].wait_send()


def on_device(tiles, object_field, probe, phases, intensities, pos_row, pos_col, counts):
    side = probe.shape[1]
    cosine, sine = angle_tables(side)
    anywhere = pl.BlockSpec(memory_space=pltpu.HBM)
    block = (2, side, side)
    wide = (2 * side, 2 * side)
    dma = pltpu.SemaphoreType.DMA
    return pl.pallas_call(
        functools.partial(kernel, tiles, side),
        out_shape=jax.ShapeDtypeStruct(object_field.shape, F32),
        in_specs=[pl.BlockSpec(memory_space=pltpu.SMEM)] + [anywhere] * 8,
        out_specs=pl.BlockSpec(memory_space=pltpu.VMEM),
        scratch_shapes=[
            pltpu.SMEM((2,), jnp.int32),
            pltpu.SMEM((2,), jnp.int32),
            pltpu.VMEM((2, side, object_field.shape[3]), BF16),
            pltpu.VMEM(block, BF16),
            pltpu.VMEM((1, side), F32),
            pltpu.VMEM((side, side), F32),
            pltpu.VMEM((side, side), F32),
            pltpu.VMEM((2, side, side), BF16),
            pltpu.VMEM((8, side), jnp.int32),
            pltpu.VMEM((8, side), jnp.int32),
            pltpu.VMEM((2,) + block, BF16),
            pltpu.VMEM((2,) + block, BF16),
            pltpu.VMEM(block, BF16),
            pltpu.VMEM(block, BF16),
            pltpu.VMEM((2,) + block, BF16),
            pltpu.VMEM((2,) + block, BF16),
            pltpu.VMEM(wide, BF16),
            pltpu.VMEM(wide, BF16),
            pltpu.VMEM((2,) + wide, BF16),
            pltpu.VMEM((2,) + wide, BF16),
            pltpu.VMEM((2,) + wide, BF16),
            pltpu.VMEM((2,) + wide, BF16),
            pltpu.VMEM((2,) + block, BF16),
            pltpu.VMEM((2 * side, side), BF16),
            pltpu.VMEM((2, 2) + block, BF16),
            pltpu.VMEM((2,) + block, BF16),
            dma((8,)),
            pltpu.SemaphoreType.REGULAR,
            dma((2,)),
            dma((2,)),
            dma((2,)),
            dma((2,)),
            dma((2,)),
            dma((2,)),
            dma((2,)),
            dma((2,)),
            dma((2,)),
            dma((2,)),
        ],
        compiler_params=pltpu.CompilerParams(
            collective_id=0, has_side_effects=True, vmem_limit_bytes=48 * 1024 * 1024
        ),
    )(
        counts,
        *(
            pltpu.with_memory_space_constraint(value, pltpu.HBM)
            for value in (
                pos_row,
                pos_col,
                object_field,
                probe,
                phases.reshape(1, side),
                intensities,
                jnp.asarray(cosine),
                jnp.asarray(sine),
            )
        )
    )


def solution(mesh):
    placed = (
        P(None, "sec", "tile", None),
        P(),
        P(),
        P("tile", None, None),
        P("tile"),
        P("tile"),
        P("tile"),
    )
    return jax.shard_map(
        functools.partial(on_device, mesh.shape["tile"]),
        mesh=mesh,
        in_specs=placed,
        out_specs=P(None, "sec", "tile", None),
        check_vma=False,
    )
```

time: 51.9 us -> 43.1 us (0.83)
  Pallas kernels: 50.1 us -> 41.3 us
    pallas_call x1, Pallas kernels: 50.1 us -> 41.3 us  [on_device(): pl.pallas_call(functools.partial(kernel, tiles, side), out_shape=jax.Shap...]
where the time goes in v3:
time: 43.1 us; the launch traced here: 42.9 us
  Pallas kernels  41.3 us (96%)
  local copies, waits for them, and re-layouts  0.97 us (2%)
  between operations  0.66 us (2%)
    pallas_call x1, Pallas kernels, on_device(): pl.pallas_call(functools.partial(kernel, tiles, side), out_shape=jax.Shap...  41.3 us
    unnamed x1, local copies, waits for them, and re-layouts  0.97 us

profile of v3, /device:TPU:1, one launch (start us, length us, event | category | flops | bytes accessed | tf_op | source)
XLA Modules:
  0.0 42.9 jit_solution(8249209530807232792)
XLA Ops:
  0.7 41.3 %shard_map.91 = f32[2,1,256,512]{3,2,1,0:T(8,128)S(1)} custom-call(s32[1]{0:T(128)S(6)} %copy.11.count_ref, s32[2]{0:T(128)} %row_hbm.1, s32[2]{0:T(128)} %col_hbm.1, bf16[2,1,256,512]{3,2,1,0:T(8,128)(2,1)} %object_hbm.1, bf16[2,256,256]{2,1,0:T(8,128)(2,1)} %probe_hbm.1, f32[1,256]{1,0:T(1,128)} %bitcast.1, bf16[2,256,256]{2,1,0:T(8,128)(2,1)} %measured_hbm.1, ...), custom_call_target="tpu_custom_call" | custom-call | tf_op jit(solution)/shard_map/pallas_call | solution.py:408
  41.9 1.0 %copy.12 = f32[2,1,256,512]{3,2,1,0:T(8,128)} copy(f32[2,1,256,512]{3,2,1,0:T(8,128)S(1)} %shard_map.91) | data formatting | bytes 2097152

commit v4 on v3

--- a/solution.py
+++ b/solution.py
@@ -76,6 +76,7 @@
     down_send,
     far_up_sem,
     far_down_sem,
+    measured_send,
     measured_sem,
     grad_send,
     grad_sem,
@@ -128,6 +129,35 @@
     def _():
         far_down[...] = jnp.zeros_like(far_down)
 
+    column = lax.broadcasted_iota(jnp.int32, (side, side), 1)
+    row = lax.broadcasted_iota(jnp.int32, (side, side), 0)
+
+    def pick(target, left_col):
+        turned = column < left_col
+        for part in range(2):
+            target[part] = jnp.where(turned, field[part, :, side:], field[part, :, :side])
+
+    to_up = [
+        remote(up.at[slot], far_up.at[sec], up_send.at[slot], far_up_sem.at[sec], (slot, after))
+        for slot in range(2)
+    ]
+    scalars = remote(mine, prev, scalar_sem.at[0], scalar_sem.at[1], (sec, after))
+    intensity = [
+        remote(
+            measured_hbm.at[slot], measured.at[1], measured_send.at[slot], measured_sem, (slot, after)
+        )
+        for slot in range(2)
+    ]
+    plane = max(tiles // 4, 3)
+    edge = (lax.rem(tile, plane) == 0) | (lax.rem(tile + 1, plane) == 0)
+    second = jnp.logical_not(first)
+    pl.semaphore_wait(barrier, jnp.where(has_next, 3, 1))
+
+    @pl.when(has_next & second)
+    def _():
+        intensity[0].start()
+        intensity[1].start()
+
     for load in loads[:2]:
         load.wait()
     line = lax.broadcasted_iota(jnp.int32, (8, side), 0)
@@ -136,43 +166,26 @@
         values = jnp.where(line == at, value, values)
     mine[...] = values
 
-    column = lax.broadcasted_iota(jnp.int32, (side, side), 1)
-    row = lax.broadcasted_iota(jnp.int32, (side, side), 0)
-
-    def pick(target, left_col):
-        turned = column < left_col
-        for part in range(2):
-            target[part] = jnp.where(turned, field[part, :, side:], field[part, :, :side])
-
-    to_up = [
-        remote(up.at[slot], far_up.at[sec], up_send.at[slot], far_up_sem.at[sec], (slot, after))
-        for slot in range(2)
-    ]
-    scalars = remote(mine, prev, scalar_sem.at[0], scalar_sem.at[1], (sec, after))
-    intensity = remote(
-        measured_hbm.at[sec], measured.at[1], measured_sem.at[0], measured_sem.at[1], (sec, after)
-    )
-    loads[2].wait()
-    pick(up.at[0], col_ref[0])
-    pl.semaphore_wait(barrier, jnp.where(has_next, 3, 1))
-
     @pl.when(has_next)
     def _():
-        to_up[0].start()
         scalars.start()
         signal(ready_sem, (other, after))
 
-    pick(up.at[1], col_ref[1])
-
-    @pl.when(has_next)
-    def _():
-        to_up[1].start()
-        intensity.start()
+    loads[2].wait()
+    for slot in range(2):
+        pick(up.at[slot], col_ref[slot])
+
+        @pl.when(has_next & (first | edge))
+        def _():
+            to_up[slot].start()
 
     to_core_up = remote(
         up.at[other], core_up, core_send.at[0], core_sem.at[0], (other, tile)
     )
-    to_core_up.start()
+
+    @pl.when(first | edge)
+    def _():
+        to_core_up.start()
 
     to_down = [
         remote(
@@ -192,6 +205,15 @@
         @pl.when(has_prev)
         def _():
             to_down[slot].start()
+
+    @pl.when(second & jnp.logical_not(edge))
+    def _():
+        to_core_up.start()
+
+        @pl.when(has_next)
+        def _():
+            to_up[0].start()
+            to_up[1].start()
 
     to_core_down = remote(
         down.at[other], core_down, core_send.at[1], core_sem.at[1], (other, tile)
@@ -268,12 +290,21 @@
     def conj_times(a_re, a_im, b_re, b_im):
         return a_re * b_re + a_im * b_im, a_re * b_im - a_im * b_re
 
-    def run(at, my_row, live, window, wait_measured):
+    to_core_grad = [
+        remote(
+            grad.at[at, other], grad_core.at[at], grad_send.at[at], grad_sem.at[at], (other, tile)
+        )
+        for at in range(2)
+    ]
+
+    def run(at, my_row, live, window, wait_layer, wait_measured):
         in_next = row < my_row
         w_re, w_im = psi0[at, 0].astype(F32), psi0[at, 1].astype(F32)
+        wait_layer(0)
         entered = transmit(window(0, in_next), w_re, w_im)
         inner = dot(entered, klt[...]).astype(BF16)
         psi1[...] = dot(kl[...], stacked(inner)).astype(BF16)
+        wait_layer(1)
         window1 = window(1, in_next)
         entered = transmit(window1, psi1[:side].astype(F32), psi1[side:].astype(F32))
         inner = dot(entered, flct[at]).astype(BF16)
@@ -294,6 +325,11 @@
         )
         grad[at, 1, 0] = grad_re.astype(BF16)
         grad[at, 1, 1] = grad_im.astype(BF16)
+
+        @pl.when(first)
+        def _():
+            to_core_grad[at].start()
+
         next_re, next_im = conj_times(window1[0], window1[1], s_re, s_im)
         entering = jnp.concatenate([next_re.astype(BF16), next_im.astype(BF16)], axis=0)
         inner = dot(klt[...], entering).astype(BF16)
@@ -301,6 +337,10 @@
         grad_re, grad_im = conj_times(w_re, w_im, spread[:, :side], spread[:, side:])
         grad[at, 0, 0] = grad_re.astype(BF16)
         grad[at, 0, 1] = grad_im.astype(BF16)
+
+        @pl.when(second)
+        def _():
+            to_core_grad[at].start()
 
     def mixed(in_next, next_block, home_block):
         return [
@@ -328,19 +368,12 @@
                 out_ref[part, 0, :, :side] += left
                 out_ref[part, 0, :, side:] += right
 
-    to_core_grad = [
-        remote(
-            grad.at[at, other], grad_core.at[at], grad_send.at[at], grad_sem.at[at], (other, tile)
-        )
-        for at in range(2)
-    ]
-
     wait_recv(core_up, core_sem.at[0])
 
-    @pl.when(has_next)
-    def _():
-        wait_recv(far_down.at[0], far_down_sem.at[0])
-        wait_recv(far_down.at[1], far_down_sem.at[1])
+    def wait_down(layer):
+        @pl.when(has_next)
+        def _():
+            wait_recv(far_down.at[layer], far_down_sem.at[layer])
 
     (my_row, my_col), (their_row, their_col), live = here
     run(
@@ -350,23 +383,23 @@
         lambda layer, in_next: mixed(
             in_next, far_down[layer], choose(layer, up[sec], core_up[...])
         ),
+        wait_down,
         lambda: None,
     )
-    to_core_grad[0].start()
     put(grad[0, sec], row >= my_row, my_col, True)
 
     (prev_row, prev_col), (prev_their_row, prev_their_col), live = there
     wait_recv(core_down, core_sem.at[1])
 
-    @pl.when(has_prev)
-    def _():
-        wait_recv(far_up.at[0], far_up_sem.at[0])
-        wait_recv(far_up.at[1], far_up_sem.at[1])
+    def wait_up(layer):
+        @pl.when(has_prev)
+        def _():
+            wait_recv(far_up.at[layer], far_up_sem.at[layer])
 
     def wait_measured():
         @pl.when(has_prev)
         def _():
-            intensity.wait_recv()
+            wait_recv(measured.at[1], measured_sem)
 
     run(
         1,
@@ -375,9 +408,9 @@
         lambda layer, in_next: mixed(
             in_next, choose(layer, down[sec], core_down[...]), far_up[layer]
         ),
+        wait_up,
         wait_measured,
     )
-    to_core_grad[1].start()
     to_core_grad[0].wait_recv()
     put(grad_core[0], row >= their_row, their_col)
     put(grad[1, sec], (row < prev_row) & has_prev, prev_col)
@@ -389,8 +422,13 @@
 
     @pl.when(has_next)
     def _():
-        for sent in (to_up[0], to_up[1], scalars, intensity):
+        for sent in (to_up[0], to_up[1], scalars):
             sent.wait_send()
+
+    @pl.when(has_next & second)
+    def _():
+        intensity[0].wait_send()
+        intensity[1].wait_send()
 
     @pl.when(has_prev)
     def _():
@@ -447,6 +485,7 @@
             dma((2,)),
             dma((2,)),
             dma((2,)),
+            dma,
             dma((2,)),
             dma((2,)),
         ],

time: 43.1 us -> 41.3 us (0.958)
  the two profiles are of different devices: /device:TPU:1 before, /device:TPU:7 now
where the time goes in v4:
time: 41.3 us; the launch traced here: 41.2 us
  Pallas kernels  39.5 us (96%)
  local copies, waits for them, and re-layouts  0.97 us (2%)
  between operations  0.66 us (2%)
    pallas_call x1, Pallas kernels, on_device(): pl.pallas_call(functools.partial(kernel, tiles, side), out_shape=jax.Shap...  39.5 us
    unnamed x1, local copies, waits for them, and re-layouts  0.97 us

profile of v4, /device:TPU:7, one launch (start us, length us, event | category | flops | bytes accessed | tf_op | source)
XLA Modules:
  0.0 41.2 jit_solution(16338620166900882831)
XLA Ops:
  0.7 39.5 %shard_map.91 = f32[2,1,256,512]{3,2,1,0:T(8,128)S(1)} custom-call(s32[1]{0:T(128)S(6)} %copy.11.count_ref, s32[2]{0:T(128)} %row_hbm.1, s32[2]{0:T(128)} %col_hbm.1, bf16[2,1,256,512]{3,2,1,0:T(8,128)(2,1)} %object_hbm.1, bf16[2,256,256]{2,1,0:T(8,128)(2,1)} %probe_hbm.1, f32[1,256]{1,0:T(1,128)} %bitcast.1, bf16[2,256,256]{2,1,0:T(8,128)(2,1)} %measured_hbm.1, ...), custom_call_target="tpu_custom_call" | custom-call | tf_op jit(solution)/shard_map/pallas_call | solution.py:446
  40.2 1.0 %copy.12 = f32[2,1,256,512]{3,2,1,0:T(8,128)} copy(f32[2,1,256,512]{3,2,1,0:T(8,128)S(1)} %shard_map.91) | data formatting | bytes 2097152

commit v5 on v4

--- a/solution.py
+++ b/solution.py
@@ -69,6 +69,7 @@
     grad_core,
     load_sem,
     ready_sem,
+    scalar_send,
     scalar_sem,
     core_send,
     core_sem,
@@ -141,7 +142,9 @@
         remote(up.at[slot], far_up.at[sec], up_send.at[slot], far_up_sem.at[sec], (slot, after))
         for slot in range(2)
     ]
-    scalars = remote(mine, prev, scalar_sem.at[0], scalar_sem.at[1], (sec, after))
+    scalars = [
+        remote(mine, prev, scalar_send.at[slot], scalar_sem, (slot, after)) for slot in range(2)
+    ]
     intensity = [
         remote(
             measured_hbm.at[slot], measured.at[1], measured_send.at[slot], measured_sem, (slot, after)
@@ -155,8 +158,9 @@
 
     @pl.when(has_next & second)
     def _():
+        signal(ready_sem, (0, after))
+        signal(ready_sem, (1, after))
         intensity[0].start()
-        intensity[1].start()
 
     for load in loads[:2]:
         load.wait()
@@ -166,10 +170,10 @@
         values = jnp.where(line == at, value, values)
     mine[...] = values
 
-    @pl.when(has_next)
-    def _():
-        scalars.start()
-        signal(ready_sem, (other, after))
+    @pl.when(has_next & first)
+    def _():
+        scalars[0].start()
+        scalars[1].start()
 
     loads[2].wait()
     for slot in range(2):
@@ -179,6 +183,10 @@
         def _():
             to_up[slot].start()
 
+    @pl.when(has_next & second & edge)
+    def _():
+        intensity[1].start()
+
     to_core_up = remote(
         up.at[other], core_up, core_send.at[0], core_sem.at[0], (other, tile)
     )
@@ -196,7 +204,7 @@
 
     @pl.when(has_prev)
     def _():
-        scalars.wait_recv()
+        remote(prev, prev, scalar_sem, scalar_sem, (other, tile)).wait_recv()
         pl.semaphore_wait(ready_sem, 1)
 
     for slot in range(2):
@@ -214,6 +222,7 @@
         def _():
             to_up[0].start()
             to_up[1].start()
+            intensity[1].start()
 
     to_core_down = remote(
         down.at[other], core_down, core_send.at[1], core_sem.at[1], (other, tile)
@@ -422,8 +431,13 @@
 
     @pl.when(has_next)
     def _():
-        for sent in (to_up[0], to_up[1], scalars):
-            sent.wait_send()
+        to_up[0].wait_send()
+        to_up[1].wait_send()
+
+    @pl.when(has_next & first)
+    def _():
+        scalars[0].wait_send()
+        scalars[1].wait_send()
 
     @pl.when(has_next & second)
     def _():
@@ -478,6 +492,7 @@
             dma((8,)),
             pltpu.SemaphoreType.REGULAR,
             dma((2,)),
+            dma,
             dma((2,)),
             dma((2,)),
             dma((2,)),

time: 41.3 us -> 40.6 us (0.983)
  the two profiles are of different devices: /device:TPU:7 before, /device:TPU:1 now
where the time goes in v5:
time: 40.6 us; the launch traced here: 39.9 us
  Pallas kernels  38.2 us (94%)
  local copies, waits for them, and re-layouts  0.97 us (2%)
  between operations  0.66 us (2%)
    pallas_call x1, Pallas kernels, on_device(): pl.pallas_call(functools.partial(kernel, tiles, side), out_shape=jax.Shap...  38.2 us
    unnamed x1, local copies, waits for them, and re-layouts  0.97 us

profile of v5, /device:TPU:1, one launch (start us, length us, event | category | flops | bytes accessed | tf_op | source)
XLA Modules:
  0.0 39.9 jit_solution(16080630093507907689)
XLA Ops:
  0.7 38.2 %shard_map.91 = f32[2,1,256,512]{3,2,1,0:T(8,128)S(1)} custom-call(s32[1]{0:T(128)S(6)} %copy.11.count_ref, s32[2]{0:T(128)} %row_hbm.1, s32[2]{0:T(128)} %col_hbm.1, bf16[2,1,256,512]{3,2,1,0:T(8,128)(2,1)} %object_hbm.1, bf16[2,256,256]{2,1,0:T(8,128)(2,1)} %probe_hbm.1, f32[1,256]{1,0:T(1,128)} %bitcast.1, bf16[2,256,256]{2,1,0:T(8,128)(2,1)} %measured_hbm.1, ...), custom_call_target="tpu_custom_call" | custom-call | tf_op jit(solution)/shard_map/pallas_call | solution.py:460
  38.9 1.0 %copy.12 = f32[2,1,256,512]{3,2,1,0:T(8,128)} copy(f32[2,1,256,512]{3,2,1,0:T(8,128)S(1)} %shard_map.91) | data formatting | bytes 2097152

commit v6 on v5

--- a/solution.py
+++ b/solution.py
@@ -209,10 +209,15 @@
 
     for slot in range(2):
         pick(down.at[slot], prev[2 + slot : 3 + slot, :])
-
-        @pl.when(has_prev)
-        def _():
-            to_down[slot].start()
+    to_core_down = remote(
+        down.at[other], core_down, core_send.at[1], core_sem.at[1], (other, tile)
+    )
+    to_core_down.start()
+
+    @pl.when(has_prev)
+    def _():
+        to_down[0].start()
+        to_down[1].start()
 
     @pl.when(second & jnp.logical_not(edge))
     def _():
@@ -223,11 +228,6 @@
             to_up[0].start()
             to_up[1].start()
             intensity[1].start()
-
-    to_core_down = remote(
-        down.at[other], core_down, core_send.at[1], core_sem.at[1], (other, tile)
-    )
-    to_core_down.start()
 
     def places(values):
         rows = (values[0:1, :], values[1:2, :])

time: 40.6 us -> 40.6 us (level)
  no operation moved by 1% of the time
where the time goes in v6:
time: 40.6 us; the launch traced here: 39.9 us
  Pallas kernels  38.2 us (94%)
  local copies, waits for them, and re-layouts  0.97 us (2%)
  between operations  0.66 us (2%)
    pallas_call x1, Pallas kernels, on_device(): pl.pallas_call(functools.partial(kernel, tiles, side), out_shape=jax.Shap...  38.2 us
    unnamed x1, local copies, waits for them, and re-layouts  0.97 us

profile of v6, /device:TPU:1, one launch (start us, length us, event | category | flops | bytes accessed | tf_op | source)
XLA Modules:
  0.0 39.9 jit_solution(10248852973566316224)
XLA Ops:
  0.7 38.2 %shard_map.91 = f32[2,1,256,512]{3,2,1,0:T(8,128)S(1)} custom-call(s32[1]{0:T(128)S(6)} %copy.11.count_ref, s32[2]{0:T(128)} %row_hbm.1, s32[2]{0:T(128)} %col_hbm.1, bf16[2,1,256,512]{3,2,1,0:T(8,128)(2,1)} %object_hbm.1, bf16[2,256,256]{2,1,0:T(8,128)(2,1)} %probe_hbm.1, f32[1,256]{1,0:T(1,128)} %bitcast.1, bf16[2,256,256]{2,1,0:T(8,128)(2,1)} %measured_hbm.1, ...), custom_call_target="tpu_custom_call" | custom-call | tf_op jit(solution)/shard_map/pallas_call | solution.py:460
  38.9 1.0 %copy.12 = f32[2,1,256,512]{3,2,1,0:T(8,128)} copy(f32[2,1,256,512]{3,2,1,0:T(8,128)S(1)} %shard_map.91) | data formatting | bytes 2097152
